TPU v7x, 32 devices: a whole 2x2x4 slice. The times are simulated.
32 devices in a mesh: grp: 16 (over z, x, core), ep: 2 (over y).
Axes of the slice: x: 2, y: 2, z: 4, core: 2. Of those that a mesh axis runs over, the one named last changes fastest.
Arguments:
- inputs: bfloat16 [8192, 1024], P(('grp', 'ep')), may hold values from -8 to 8
- attn_gain: bfloat16 [1024], P(('grp', 'ep')), may hold values from 0.099609375 to 1.8984375
- w_query: bfloat16 [1024, 1024], P(('grp', 'ep')), may hold values from -0.1875 to 0.1875
- w_key: bfloat16 [1024, 1024], P(('grp', 'ep')), may hold values from -0.1875 to 0.1875
- w_value: bfloat16 [1024, 1024], P(('grp', 'ep')), may hold values from -0.25 to 0.25
- w_output: bfloat16 [1024, 1024], P(('grp', 'ep')), may hold values from -3 to 3
- centroids: bfloat16 [1024, 2], P(('grp', 'ep')), may hold values from -0.09375 to 0.09375
- norm1_gain: bfloat16 [2, 1024], P('ep'), may hold values from 0.099609375 to 1.8984375
- norm2_gain: bfloat16 [2, 1024], P('ep'), may hold values from 0.099609375 to 1.8984375
- up_first: bfloat16 [2, 1024, 4096], P('ep'), may hold values from -0.1875 to 0.1875
- down_first: bfloat16 [2, 4096, 1024], P('ep'), may hold values from -0.09375 to 0.09375
- up_second: bfloat16 [2, 1024, 4096], P('ep'), may hold values from -0.1875 to 0.1875
- down_second: bfloat16 [2, 4096, 1024], P('ep'), may hold values from -0.09375 to 0.09375
- routes: int32 [8192, 1], P(('grp', 'ep')), may hold values from 0 to 1; in each aligned block of 256 rows (0 to 255, 256 to 511, ...) at most 256 rows name the same one
- prefix: int32 [32], P(('grp', 'ep')), may hold values from 25 to 128
- cotangent: bfloat16 [8192, 1024], P(('grp', 'ep')), may hold values from -6 to 6
Outputs:
- output: bfloat16 [8192, 1024], P(('grp', 'ep'))
- input_grad: float32 [8192, 1024], P(('grp', 'ep'))
- attn_gain_grad: float32 [1024], P(('grp', 'ep'))
- query_grad: float32 [1024, 1024], P(('grp', 'ep'))
- key_grad: float32 [1024, 1024], P(('grp', 'ep'))
- value_grad: float32 [1024, 1024], P(('grp', 'ep'))
- out_proj_grad: float32 [1024, 1024], P(('grp', 'ep'))
- centroid_grad: float32 [1024, 2], P(('grp', 'ep'))
- norm1_grad: float32 [2, 1024], P('ep', 'grp')
- norm2_grad: float32 [2, 1024], P('ep', 'grp')
- up_first_grad: float32 [2, 1024, 4096], P('ep', None, 'grp')
- down_first_grad: float32 [2, 4096, 1024], P('ep', 'grp')
- up_second_grad: float32 [2, 1024, 4096], P('ep', None, 'grp')
- down_second_grad: float32 [2, 4096, 1024], P('ep', 'grp')
- rms_values: float32 [4], replicated
Inputs may be any that keep to these rules, and one draw needn't show every extreme that they name: `routes`: in the rows of one sequence no expert is named by more than 256 rows; in some sequence one expert is named by exactly 256.
All inputs are finite; a program needn't handle non-finite values.
Results may differ from a plain program's by a relative error of at most 0.012.
The roundings to bfloat16 on the way count: a program that leaves them out, or rounds other values in their place, can miss the bound.
Values may be sent and summed in bfloat16 or wider, within the bound.
A program may use at most 256 MiB of HBM per device.

v0:
```python
import jax
import jax.numpy as jnp
from jax import lax
from jax.sharding import PartitionSpec as P

HEADS = 16


EPSILON = 1e-05
SQRT_HALF = 0.7071067811865476
INV_ROOT_TWO_PI = 0.3989422804014327
HIGH = lax.Precision.HIGHEST


def norm_parts(rows_in):
    center = rows_in - jnp.mean(rows_in, axis=-1, keepdims=True)
    inverse = lax.rsqrt(jnp.mean(center * center, axis=-1, keepdims=True) + EPSILON)
    return (center * inverse, inverse)


def norm_back(grad_normed, normed, inverse):
    mean_grad = jnp.mean(grad_normed, axis=-1, keepdims=True)
    mean_dot = jnp.mean(grad_normed * normed, axis=-1, keepdims=True)
    return inverse * (grad_normed - mean_grad - normed * mean_dot)


def gelu_slope(preact):
    return (
        0.5 * (1.0 + jax.scipy.special.erf(preact * SQRT_HALF))
        + preact * jnp.exp(-0.5 * preact * preact) * INV_ROOT_TWO_PI
    )


def matmul(left_side, right_side):
    return jnp.dot(left_side, right_side, preferred_element_type=jnp.float32)


def dot_first(left_side, right_side):
    return lax.dot_general(
        left_side, right_side, (((0,), (0,)), ((), ())), preferred_element_type=jnp.float32
    )


def dot_last(left_side, right_side):
    return lax.dot_general(
        left_side, right_side, (((1,), (1,)), ((), ())), preferred_element_type=jnp.float32
    )


def visible_mask(row_start, row_count, key_count, prefix_len):
    row_ids = row_start + jnp.arange(row_count, dtype=jnp.int32)[:, None]
    col_ids = jnp.arange(key_count, dtype=jnp.int32)[None, :]
    return (col_ids <= row_ids) | (col_ids < prefix_len)


def fill_slots(rows_in, target, slot_total):
    return jnp.zeros((slot_total, rows_in.shape[1]), rows_in.dtype).at[target].set(rows_in)


def shards(
    inputs,
    attn_gain,
    w_query,
    w_key,
    w_value,
    w_output,
    centroids,
    norm1_gain,
    norm2_gain,
    up_first,
    down_first,
    up_second,
    down_second,
    routes,
    prefix,
    cotangent,
):
    gathered = (
        lax.all_gather(attn_gain, ("grp", "ep"), axis=0, tiled=True),
        lax.all_gather(w_query, ("grp", "ep"), axis=0, tiled=True),
        lax.all_gather(w_key, ("grp", "ep"), axis=0, tiled=True),
        lax.all_gather(w_value, ("grp", "ep"), axis=0, tiled=True),
        lax.all_gather(w_output, ("grp", "ep"), axis=0, tiled=True),
        lax.all_gather(centroids, ("grp", "ep"), axis=0, tiled=True),
    )
    gain_attn, query_mat, key_mat, value_mat, output_mat, centroid_mat = gathered
    token_count, feature_width = inputs.shape
    head_count = HEADS
    head_width = feature_width // head_count
    scale_factor = head_width ** (-0.5)
    block_rows = min(512, token_count)
    prefix_len = prefix[0]
    inputs_wide = inputs.astype(jnp.float32)
    normed_attn, inverse_attn = norm_parts(inputs_wide)
    gain_attn_wide = gain_attn.astype(jnp.float32)
    attn_in = (normed_attn * gain_attn_wide).astype(jnp.bfloat16)
    queries = (
        matmul(attn_in, query_mat).astype(jnp.bfloat16).reshape(token_count, head_count, head_width)
    )
    key_heads = (
        matmul(attn_in, key_mat).astype(jnp.bfloat16).reshape(token_count, head_count, head_width)
    )
    value_heads = (
        matmul(attn_in, value_mat).astype(jnp.bfloat16).reshape(token_count, head_count, head_width)
    )

    def block_scores(block_index):
        row_start = block_index * block_rows
        scores = (
            jnp.einsum("qhd,khd->hqk", queries, key_heads, preferred_element_type=jnp.float32)
            * scale_factor
        )
        visible = visible_mask(row_start, block_rows, token_count, prefix_len)
        return (queries, jnp.where(visible[None], scores, -1e30))

    block_index = 0
    query_block, scores = block_scores(block_index)
    row_max = jnp.max(scores, axis=-1, keepdims=True)
    expsum = jnp.sum(jnp.exp(scores - row_max), axis=-1, keepdims=True)
    log_total = row_max + jnp.log(expsum)
    probs_low = jnp.exp(scores - log_total).astype(jnp.bfloat16)
    context_parts = jnp.einsum(
        "hqk,khd->qhd", probs_low, value_heads, preferred_element_type=jnp.float32
    ).astype(jnp.bfloat16)
    lse_parts = [log_total]
    context = context_parts.reshape(token_count, feature_width)
    branch = matmul(context, output_mat)
    hidden = inputs_wide + branch
    hidden_low = hidden.astype(jnp.bfloat16)
    expert_total = lax.axis_size("ep")
    group_total = lax.axis_size("grp")
    capacity = 2 * token_count // expert_total
    route_ids = routes[:, 0]
    expert_ids = jnp.arange(expert_total, dtype=jnp.int32)
    route_hot = (route_ids[:, None] == expert_ids[None, :]).astype(jnp.int32)
    position = jnp.sum((jnp.cumsum(route_hot, axis=0) - 1) * route_hot, axis=1)
    target = route_ids * capacity + position
    route_weight = route_hot.astype(jnp.float32)
    all_scores = matmul(hidden_low, centroid_mat)
    gate_value = jax.nn.sigmoid(jnp.sum(all_scores * route_weight, axis=1))
    slot_rows = fill_slots(hidden_low, target, expert_total * capacity).reshape(
        expert_total, capacity, feature_width
    )
    received = lax.all_to_all(slot_rows, "ep", split_axis=0, concat_axis=0, tiled=True).reshape(
        expert_total * capacity, feature_width
    )
    gain_one = norm1_gain[0].astype(jnp.float32)
    gain_two = norm2_gain[0].astype(jnp.float32)
    up_one = up_first[0]
    down_one = down_first[0]
    up_two = up_second[0]
    down_two = down_second[0]
    rows_wide = received.astype(jnp.float32)
    normed_one, inverse_one = norm_parts(rows_wide)
    in_one = (normed_one * gain_one).astype(jnp.bfloat16)
    pre_one = matmul(in_one, up_one)
    act_one = jax.nn.gelu(pre_one, approximate=False).astype(jnp.bfloat16)
    sub_one = matmul(act_one, down_one)
    middle = rows_wide + sub_one
    normed_two, inverse_two = norm_parts(middle)
    in_two = (normed_two * gain_two).astype(jnp.bfloat16)
    pre_two = matmul(in_two, up_two)
    act_two = jax.nn.gelu(pre_two, approximate=False).astype(jnp.bfloat16)
    sub_two = matmul(act_two, down_two)
    delta = (sub_one + sub_two).astype(jnp.bfloat16).reshape(expert_total, capacity, feature_width)
    back_slots = lax.all_to_all(delta, "ep", split_axis=0, concat_axis=0, tiled=True).reshape(
        expert_total * capacity, feature_width
    )
    returned = back_slots[target].astype(jnp.float32)
    result = hidden + gate_value[:, None] * returned
    square_terms = jnp.stack(
        [
            jnp.sum(result * result),
            jnp.sum(branch * branch),
            jnp.sum(sub_one * sub_one),
            jnp.sum(sub_two * sub_two),
        ]
    )
    square_totals = lax.psum(square_terms, ("grp", "ep"))
    cell_count = float(token_count * feature_width * group_total * expert_total)
    rms_values = jnp.sqrt(square_totals / cell_count)
    grad_out = cotangent.astype(jnp.float32)
    grad_gate = jnp.sum(grad_out * returned, axis=1)
    grad_score = grad_gate * gate_value * (1.0 - gate_value)
    grad_delta_tok = (gate_value[:, None] * grad_out).astype(jnp.bfloat16)
    grad_slots = fill_slots(grad_delta_tok, target, expert_total * capacity).reshape(
        expert_total, capacity, feature_width
    )
    grad_sum = lax.all_to_all(grad_slots, "ep", split_axis=0, concat_axis=0, tiled=True).reshape(
        expert_total * capacity, feature_width
    )
    grad_pre_two = (dot_last(grad_sum, down_two) * gelu_slope(pre_two)).astype(jnp.bfloat16)
    grad_in_two = dot_last(grad_pre_two, up_two)
    grad_gain_two = jnp.sum(grad_in_two * normed_two, axis=0)
    grad_middle = norm_back(grad_in_two * gain_two, normed_two, inverse_two)
    grad_sub_one = (grad_sum.astype(jnp.float32) + grad_middle).astype(jnp.bfloat16)
    grad_pre_one = (dot_last(grad_sub_one, down_one) * gelu_slope(pre_one)).astype(jnp.bfloat16)
    grad_in_one = dot_last(grad_pre_one, up_one)
    grad_gain_one = jnp.sum(grad_in_one * normed_one, axis=0)
    grad_rows = (norm_back(grad_in_one * gain_one, normed_one, inverse_one) + grad_middle).astype(
        jnp.bfloat16
    )
    grad_back = lax.all_to_all(
        grad_rows.reshape(expert_total, capacity, feature_width),
        "ep",
        split_axis=0,
        concat_axis=0,
        tiled=True,
    ).reshape(expert_total * capacity, feature_width)
    grad_down_two = dot_first(act_two, grad_sum)
    grad_up_two = dot_first(in_two, grad_pre_two)
    grad_down_one = dot_first(act_one, grad_sub_one)
    grad_up_one = dot_first(in_one, grad_pre_one)
    expert_sums = (
        lax.psum_scatter(grad_up_one[None], "grp", scatter_dimension=2, tiled=True),
        lax.psum_scatter(grad_down_one[None], "grp", scatter_dimension=1, tiled=True),
        lax.psum_scatter(grad_up_two[None], "grp", scatter_dimension=2, tiled=True),
        lax.psum_scatter(grad_down_two[None], "grp", scatter_dimension=1, tiled=True),
        lax.psum_scatter(grad_gain_one[None], "grp", scatter_dimension=1, tiled=True),
        lax.psum_scatter(grad_gain_two[None], "grp", scatter_dimension=1, tiled=True),
    )
    up_one_sum, down_one_sum, up_two_sum, down_two_sum, gain_one_sum, gain_two_sum = expert_sums
    centroid_wide = centroid_mat.astype(jnp.float32)
    score_weight = route_weight * grad_score[:, None]
    grad_hidden = (
        grad_out
        + jnp.dot(score_weight, centroid_wide.T, precision=HIGH)
        + grad_back[target].astype(jnp.float32)
    )
    grad_centroid = lax.dot_general(
        hidden_low.astype(jnp.float32), score_weight, (((0,), (0,)), ((), ())), precision=HIGH
    )
    grad_branch = grad_hidden.astype(jnp.bfloat16)
    grad_output_mat = dot_first(context, grad_branch)
    grad_context = (
        dot_last(grad_branch, output_mat)
        .astype(jnp.bfloat16)
        .reshape(token_count, head_count, head_width)
    )
    block_index = 0
    query_block, scores = block_scores(block_index)
    probs_wide = jnp.exp(scores - lse_parts[block_index])
    probs_low = probs_wide.astype(jnp.bfloat16)
    row_start = block_index * block_rows
    grad_value_sum = jnp.einsum(
        "hqk,qhd->khd", probs_low, grad_context, preferred_element_type=jnp.float32
    )
    grad_probs = jnp.einsum(
        "qhd,khd->hqk", grad_context, value_heads, preferred_element_type=jnp.float32
    )
    row_dot = jnp.sum(grad_probs * probs_wide, axis=-1, keepdims=True)
    grad_scores = (probs_wide * (grad_probs - row_dot)).astype(jnp.bfloat16)
    grad_query_parts = (
        jnp.einsum("hqk,khd->qhd", grad_scores, key_heads, preferred_element_type=jnp.float32)
        * scale_factor
    ).astype(jnp.bfloat16)
    grad_key_sum = (
        jnp.einsum("hqk,qhd->khd", grad_scores, query_block, preferred_element_type=jnp.float32)
        * scale_factor
    )
    grad_queries = grad_query_parts.reshape(token_count, feature_width)
    grad_keys = grad_key_sum.astype(jnp.bfloat16).reshape(token_count, feature_width)
    grad_values = grad_value_sum.astype(jnp.bfloat16).reshape(token_count, feature_width)
    grad_query_mat = dot_first(attn_in, grad_queries)
    grad_key_mat = dot_first(attn_in, grad_keys)
    grad_value_mat = dot_first(attn_in, grad_values)
    grad_attn_in = (
        dot_last(grad_queries, query_mat)
        + dot_last(grad_keys, key_mat)
        + dot_last(grad_values, value_mat)
    )
    grad_gain_attn = jnp.sum(grad_attn_in * normed_attn, axis=0)
    input_grad = grad_hidden + norm_back(grad_attn_in * gain_attn_wide, normed_attn, inverse_attn)
    attn_terms = (
        grad_gain_attn,
        grad_query_mat,
        grad_key_mat,
        grad_value_mat,
        grad_output_mat,
        grad_centroid,
    )
    outer_sums = (
        lax.psum_scatter(attn_terms[0], "grp", scatter_dimension=0, tiled=True),
        lax.psum_scatter(attn_terms[1], "grp", scatter_dimension=0, tiled=True),
        lax.psum_scatter(attn_terms[2], "grp", scatter_dimension=0, tiled=True),
        lax.psum_scatter(attn_terms[3], "grp", scatter_dimension=0, tiled=True),
        lax.psum_scatter(attn_terms[4], "grp", scatter_dimension=0, tiled=True),
        lax.psum_scatter(attn_terms[5], "grp", scatter_dimension=0, tiled=True),
    )
    attn_sums = (
        lax.psum_scatter(outer_sums[0], "ep", scatter_dimension=0, tiled=True),
        lax.psum_scatter(outer_sums[1], "ep", scatter_dimension=0, tiled=True),
        lax.psum_scatter(outer_sums[2], "ep", scatter_dimension=0, tiled=True),
        lax.psum_scatter(outer_sums[3], "ep", scatter_dimension=0, tiled=True),
        lax.psum_scatter(outer_sums[4], "ep", scatter_dimension=0, tiled=True),
        lax.psum_scatter(outer_sums[5], "ep", scatter_dimension=0, tiled=True),
    )
    return (
        result.astype(jnp.bfloat16),
        input_grad,
        attn_sums[0],
        attn_sums[1],
        attn_sums[2],
        attn_sums[3],
        attn_sums[4],
        attn_sums[5],
        gain_one_sum,
        gain_two_sum,
        up_one_sum,
        down_one_sum,
        up_two_sum,
        down_two_sum,
        rms_values,
    )


def solution(mesh):
    in_specs = (
        P(("grp", "ep"), None),
        P(("grp", "ep")),
        P(("grp", "ep"), None),
        P(("grp", "ep"), None),
        P(("grp", "ep"), None),
        P(("grp", "ep"), None),
        P(("grp", "ep"), None),
        P("ep", None),
        P("ep", None),
        P("ep", None, None),
        P("ep", None, None),
        P("ep", None, None),
        P("ep", None, None),
        P(("grp", "ep"), None),
        P(("grp", "ep")),
        P(("grp", "ep"), None),
    )
    out_specs = (
        P(("grp", "ep"), None),
        P(("grp", "ep"), None),
        P(("grp", "ep")),
        P(("grp", "ep"), None),
        P(("grp", "ep"), None),
        P(("grp", "ep"), None),
        P(("grp", "ep"), None),
        P(("grp", "ep"), None),
        P("ep", "grp"),
        P("ep", "grp"),
        P("ep", None, "grp"),
        P("ep", "grp", None),
        P("ep", None, "grp"),
        P("ep", "grp", None),
        P(),
    )
    return jax.shard_map(shards, mesh=mesh, in_specs=in_specs, out_specs=out_specs, check_vma=False)
```

profile of v0, /device:TPU:1, one launch (start us, length us, event | category | flops | bytes accessed | tf_op | source)
XLA Modules:
  0.0 1755.8 jit_solution(1676221756305687057)
XLA Ops:
  13.2 40.6 %all-reduce = bf16[1024]{0:T(1024)(128)(2,1)S(1)} all-reduce(bf16[1024]{0:T(1024)(128)(2,1)S(1)} %dynamic-update-slice), channel_id=1, replica_groups=mesh['grp'=16,'ep'=2] {'grp','ep'}, use_global_device_ids=true, to_apply=%add | all-reduce | flops 1024 | bytes 4096
  58.1 12.1 all-gather.10.cloned.1.call-done
  72.9 55.8 %all-gather.8.cloned.1.call-done = bf16[1024,1024]{1,0:T(8,128)(2,1)} async-done(((bf16[32,1024]{1,0:T(8,128)(2,1)}), bf16[1024,1024]{1,0:T(8,128)(2,1)}) %all-gather.8.cloned.1.call-update) | async-done | bytes 2097168 | tf_op jit(solution)/shard_map/all_gather | solution.py:80
  131.5 55.7 %all-gather.6.cloned.1.call-done = bf16[1024,1024]{1,0:T(8,128)(2,1)} async-done(((bf16[32,1024]{1,0:T(8,128)(2,1)}), bf16[1024,1024]{1,0:T(8,128)(2,1)}) %all-gather.6.cloned.1.call-update) | async-done | bytes 2097168 | tf_op jit(solution)/shard_map/all_gather | solution.py:82
  193.8 51.8 %all-gather.12.cloned.1.call-done = bf16[1024,1024]{1,0:T(8,128)(2,1)} async-done(((bf16[32,1024]{1,0:T(8,128)(2,1)}), bf16[1024,1024]{1,0:T(8,128)(2,1)}) %all-gather.12.cloned.1.call-update) | async-done | bytes 2097168 | tf_op jit(solution)/shard_map/all_gather | solution.py:83
  245.6 3.3 fusion.91
  251.5 3.8 all-to-all-start
  255.3 13.4 all-to-all-done
  270.9 25.0 %fusion.2 = (bf16[512,4096]{1,0:T(8,128)(2,1)S(1)}, f32[512,4096]{1,0:T(8,128)}) fusion(bf16[512,1024]{1,0:T(8,128)(2,1)S(1)} %bitcast.211, bf16[1,1024,4096]{2,1,0:T(8,128)(2,1)} %param.25), kind=kOutput, calls=%fused_computation.14 | convolution fusion | flops 4431282176 | bytes 22020096 | tf_op jit(solution)/shard_map/dot_general | solution.py:35
  296.0 4.6 fusion.127
  301.0 24.7 %fusion.5 = (bf16[512,4096]{1,0:T(8,128)(2,1)S(1)}, f32[512,4096]{1,0:T(8,128)}) fusion(bf16[1,1024,4096]{2,1,0:T(8,128)(2,1)S(1)} %bitcast.244, f32[512,1024]{1,0:T(8,128)S(1)} %get-tuple-element.32, f32[1024]{0:T(1024)S(1)} %bitcast.217, f32[512]{0:T(512)S(1)} %add_rsqrt_fusion, f32[512]{0:T(512)S(1)} %broadcast_multiply_fusion.4), kind=kOutput, calls=%fused_computation.17 | convolution fusion | flops 4433379328 | bytes 23076864 | tf_op jit(solution)/shard_map/dot_general | solution.py:35
  325.8 6.1 multiply_reduce_fusion.2
  331.9 3.7 all-to-all-start.1
  335.7 68.0 %all-gather = bf16[32,32,2]{1,2,0:T(2,128)(2,1)S(1)} all-gather(bf16[1,32,2]{1,2,0:T(2,128)(2,1)S(1)} %bitcast.240), channel_id=1, replica_groups=mesh['grp'=16,'ep'=2] {'grp','ep'}, dimensions={0}, use_global_device_ids=true | all-gather | bytes 4224 | tf_op jit(solution)/shard_map/all_gather | solution.py:84
  405.5 3.1 scatter_custom_fusion.1
  408.6 3.6 all-to-all-start.2
  412.3 10.2 all-to-all-done.2
  423.4 10.5 fusion.11
  433.9 9.0 multiply_reduce_fusion.3
  443.9 11.1 fusion.17
  455.0 5.9 fusion.69
  463.2 3.6 all-to-all-start.3
  469.5 6.6 all-to-all-done.3
  478.0 3.0 fusion.71
  481.0 4.0 fusion.98
  485.1 3.5 convolution_convert_fusion.1
  490.7 3.4 convolution_convert_fusion
  494.9 2.9 fusion.118
  498.1 4.0 multiply_reduce_fusion
  512.9 2.8 fusion.122
  515.8 10.3 reduce-scatter.49.cloned.1.call-done
  528.5 73.7 %reduce-scatter.37.cloned.1.call-done = f32[64,1024]{1,0:T(8,128)} async-done(((f32[1024,1024]{1,0:T(8,128)}), f32[64,1024]{1,0:T(8,128)}) %reduce-scatter.37.cloned.1.call-update) | async-done | bytes 262160 | tf_op jit(solution)/shard_map/reduce_scatter | solution.py:287
  602.3 75.4 %reduce-scatter.33.cloned.1.call-done = f32[64,1024]{1,0:T(8,128)} async-done(((f32[1024,1024]{1,0:T(8,128)}), f32[64,1024]{1,0:T(8,128)}) %reduce-scatter.33.cloned.1.call-update) | async-done | bytes 262160 | tf_op jit(solution)/shard_map/reduce_scatter | solution.py:286
  677.7 75.8 %reduce-scatter.29.cloned.1.call-done = f32[64,1024]{1,0:T(8,128)} async-done(((f32[1024,1024]{1,0:T(8,128)}), f32[64,1024]{1,0:T(8,128)}) %reduce-scatter.29.cloned.1.call-update) | async-done | bytes 262160 | tf_op jit(solution)/shard_map/reduce_scatter | solution.py:285
  753.6 75.3 %reduce-scatter.25.cloned.1.call-done = f32[64,1024]{1,0:T(8,128)} async-done(((f32[1024,1024]{1,0:T(8,128)}), f32[64,1024]{1,0:T(8,128)}) %reduce-scatter.25.cloned.1.call-update) | async-done | bytes 262160 | tf_op jit(solution)/shard_map/reduce_scatter | solution.py:284
  828.9 10.5 convolution_bitcast_fusion.1
  840.6 10.4 convolution_bitcast_fusion.2
  852.2 10.4 convolution_bitcast_fusion.3
  863.9 10.5 convolution_bitcast_fusion
  878.8 20.6 %reduce-scatter.55.cloned.1.call-done = f32[64,1]{1,0:T(8,128)} async-done(((f32[1024,1]{1,0:T(8,128)}), f32[64,1]{1,0:T(8,128)}) %reduce-scatter.55.cloned.1.call-update) | async-done | bytes 272
  911.0 46.6 %reduce-scatter.53.cloned.1.call-done = f32[64,1]{1,0:T(8,128)} async-done(((f32[1024,1]{1,0:T(8,128)}), f32[64,1]{1,0:T(8,128)}) %reduce-scatter.53.cloned.1.call-update) | async-done | bytes 272
  959.0 42.0 %psum.7 = f32[4]{0:T(128)S(1)} all-reduce(f32[4]{0:T(128)S(1)} %pad_maximum_fusion), channel_id=1, replica_groups=mesh['grp'=16,'ep'=2] {'grp','ep'}, use_global_device_ids=true, to_apply=%region_47.48 | all-reduce | flops 4 | bytes 32 | tf_op jit(solution)/shard_map/psum | solution.py:179
  1001.0 29.5 %all-reduce.1 = f32[1024]{0:T(1024)S(1)} all-reduce(f32[1024]{0:T(1024)S(1)} %get-tuple-element.28), channel_id=2, replica_groups=mesh['grp'=16,'ep'=2] {'grp'}, use_global_device_ids=true, to_apply=%region_23.24.clone | all-reduce | flops 1024 | bytes 8192
  1030.6 4.3 all-reduce.2
  1038.8 161.7 %reduce-scatter.45.cloned.1.call-done = f32[1,1024,256]{2,1,0:T(8,128)} async-done(((f32[1,1024,4096]{2,1,0:T(8,128)}), f32[1,1024,256]{2,1,0:T(8,128)}) %reduce-scatter.45.cloned.1.call-update) | async-done | bytes 1048592 | tf_op jit(solution)/shard_map/reduce_scatter | solution.py:217
  1200.4 182.7 %reduce-scatter.43.cloned.1.call-done = f32[1,256,1024]{2,1,0:T(8,128)} async-done(((f32[1,4096,1024]{2,1,0:T(8,128)}), f32[1,256,1024]{2,1,0:T(8,128)}) %reduce-scatter.43.cloned.1.call-update) | async-done | bytes 1048592 | tf_op jit(solution)/shard_map/reduce_scatter | solution.py:216
  1383.1 182.8 %reduce-scatter.41.cloned.1.call-done = f32[1,1024,256]{2,1,0:T(8,128)} async-done(((f32[1,1024,4096]{2,1,0:T(8,128)}), f32[1,1024,256]{2,1,0:T(8,128)}) %reduce-scatter.41.cloned.1.call-update) | async-done | bytes 1048592 | tf_op jit(solution)/shard_map/reduce_scatter | solution.py:215
  1565.9 182.7 %reduce-scatter.47.cloned.1.call-done = f32[1,256,1024]{2,1,0:T(8,128)} async-done(((f32[1,4096,1024]{2,1,0:T(8,128)}), f32[1,256,1024]{2,1,0:T(8,128)}) %reduce-scatter.47.cloned.1.call-update) | async-done | bytes 1048592 | tf_op jit(solution)/shard_map/reduce_scatter | solution.py:218
  (251 shorter events, 77.5 us)
Async XLA Ops:
  7.2 180.0 %copy-start.2 = (bf16[256,1024]{1,0:T(8,128)(2,1)S(1)}, bf16[256,1024]{1,0:T(8,128)(2,1)}, u32[]{:S(2)}) copy-start(bf16[256,1024]{1,0:T(8,128)(2,1)} %param.16) | copy-start | bytes 1572868
  7.2 63.0 %all-gather.10.cloned.1.call-start = ((), (), s32[]{:S(2)}) async-start(), calls=%async_computation.22 | async-start | bytes 2162688 | tf_op jit(solution)/shard_map/all_gather | solution.py:81
  7.9 120.8 %all-gather.8.cloned.1.call-start = ((), (), s32[]{:S(2)}) async-start(), calls=%async_computation.21 | async-start | bytes 2162688 | tf_op jit(solution)/shard_map/all_gather | solution.py:80
  8.7 178.5 %all-gather.6.cloned.1.call-start = ((), (), s32[]{:S(2)}) async-start(), calls=%async_computation.20 | async-start | bytes 2162688 | tf_op jit(solution)/shard_map/all_gather | solution.py:82
  9.4 236.1 %all-gather.12.cloned.1.call-start = ((), (), s32[]{:S(2)}) async-start(), calls=%async_computation.23 | async-start | bytes 2162688 | tf_op jit(solution)/shard_map/all_gather | solution.py:83
  53.8 136.8 %copy-start.33 = (f32[1024]{0:T(1024)}, f32[1024]{0:T(1024)S(1)}, u32[]{:S(2)}) copy-start(f32[1024]{0:T(1024)S(1)} %convert_element_type.136) | copy-start | bytes 12292
  55.9 134.7 %copy-start.38 = (f32[256]{0:T(256)}, f32[256]{0:T(256)S(1)}, u32[]{:S(2)}) copy-start(f32[256]{0:T(256)S(1)} %broadcast_multiply_fusion.8) | copy-start | bytes 3076
  57.3 133.4 %copy-start.40 = (f32[256]{0:T(256)}, f32[256]{0:T(256)S(1)}, u32[]{:S(2)}) copy-start(f32[256]{0:T(256)S(1)} %add_rsqrt_fusion.2) | copy-start | bytes 3076
  58.0 190.9 %copy-start.44 = (s32[256,1]{0,1:T(1,128)}, s32[256,1]{0,1:T(1,128)S(1)}, u32[]{:S(2)}) copy-start(s32[256,1]{0,1:T(1,128)S(1)} %compare_select_fusion) | copy-start | bytes 3076
  58.1 133.5 %copy-start.23 = (pred[256,256]{0,1:T(8,128)(4,1)}, pred[256,256]{0,1:T(8,128)(4,1)S(1)}, u32[]{:S(2)}) copy-start(pred[256,256]{0,1:T(8,128)(4,1)S(1)} %fusion.101) | copy-start | bytes 196612
  72.9 118.6 %copy-start.11 = (bf16[256,1024]{0,1:T(8,128)(2,1)}, bf16[256,1024]{0,1:T(8,128)(2,1)S(1)}, u32[]{:S(2)}) copy-start(bf16[256,1024]{0,1:T(8,128)(2,1)S(1)} %copy.54) | copy-start | bytes 1572868
  131.5 62.3 %copy-start.12 = (bf16[256,1024]{0,1:T(8,128)(2,1)}, bf16[256,1024]{0,1:T(8,128)(2,1)S(1)}, u32[]{:S(2)}) copy-start(bf16[256,1024]{0,1:T(8,128)(2,1)S(1)} %copy.53) | copy-start | bytes 1572868
  189.8 59.1 %copy-start.20 = (bf16[256,1024]{0,1:T(8,128)(2,1)}, bf16[256,1024]{0,1:T(8,128)(2,1)S(1)}, u32[]{:S(2)}) copy-start(bf16[256,1024]{0,1:T(8,128)(2,1)S(1)} %copy.52) | copy-start | bytes 1572868
  190.7 64.6 %copy-start.46 = (bf16[1,1024]{1,0:T(2,128)(2,1)S(1)}, bf16[1,1024]{1,0:T(2,128)(2,1)}, u32[]{:S(2)}) copy-start(bf16[1,1024]{1,0:T(2,128)(2,1)} %param.23) | copy-start | bytes 6148
  190.7 64.6 %copy-start.47 = (bf16[1,1024]{1,0:T(2,128)(2,1)S(1)}, bf16[1,1024]{1,0:T(2,128)(2,1)}, u32[]{:S(2)}) copy-start(bf16[1,1024]{1,0:T(2,128)(2,1)} %param.24) | copy-start | bytes 6148
  193.8 102.2 %copy-start.22 = (bf16[16,64,256]{2,1,0:T(8,128)(2,1)}, bf16[16,64,256]{2,1,0:T(8,128)(2,1)S(1)}, u32[]{:S(2)}) copy-start(bf16[16,64,256]{2,1,0:T(8,128)(2,1)S(1)} %convolution_convert_fusion.2) | copy-start | bytes 1572868
  251.5 17.2 all-to-all-start
  255.3 40.7 %copy-start.35 = (f32[1,1024]{1,0:T(1,128)}, f32[1,1024]{1,0:T(1,128)S(1)}, u32[]{:S(2)}) copy-start(f32[1,1024]{1,0:T(1,128)S(1)} %mul.379) | copy-start | bytes 12292
  268.7 32.3 %slice-start.2 = ((s8[8388608]{0:T(1024)(128)(4,1)}), s8[4194304]{0:T(1024)(128)(4,1)S(1)}, s32[]{:S(2)}) async-start(s8[8388608]{0:T(1024)(128)(4,1)} %bitcast.243), calls=%async_computation.42 | async-start | bytes 8388608
  270.9 30.1 %slice-start.3 = ((s8[8388608]{0:T(1024)(128)(4,1)}), s8[4194304]{0:T(1024)(128)(4,1)S(1)}, s32[]{:S(2)}) async-start(s8[8388608]{0:T(1024)(128)(4,1)} %bitcast.243), calls=%async_computation.43 | async-start | bytes 8388608
  296.0 29.7 %slice-start = ((s8[8388608]{0:T(1024)(128)(4,1)}), s8[4194304]{0:T(1024)(128)(4,1)S(1)}, s32[]{:S(2)}) async-start(s8[8388608]{0:T(1024)(128)(4,1)} %bitcast.241), calls=%async_computation.40 | async-start | bytes 8388608
  325.8 78.0 %copy-start.45 = (s32[256,1]{0,1:T(1,128)S(1)}, s32[256,1]{0,1:T(1,128)}, u32[]{:S(2)}) copy-start(s32[256,1]{0,1:T(1,128)} %copy-done.44) | copy-start | bytes 3076
  325.8 78.0 %copy-start.8 = (bf16[256,1024]{1,0:T(8,128)(2,1)S(1)}, bf16[256,1024]{1,0:T(8,128)(2,1)}, u32[]{:S(2)}) copy-start(bf16[256,1024]{1,0:T(8,128)(2,1)} %copy-done.7) | copy-start | bytes 1572868
  325.8 78.0 %copy-start.37 = (s32[256,1]{0,1:T(1,128)S(1)}, s32[256,1]{0,1:T(1,128)}, u32[]{:S(2)}) copy-start(s32[256,1]{0,1:T(1,128)} %param.29) | copy-start | bytes 3076
  325.8 79.5 %copy-start.6 = (bf16[256,1024]{1,0:T(8,128)(2,1)S(1)}, bf16[256,1024]{1,0:T(8,128)(2,1)}, u32[]{:S(2)}) copy-start(bf16[256,1024]{1,0:T(8,128)(2,1)} %param.31) | copy-start | bytes 1572868
  331.9 80.3 %copy-start.42 = (f32[1,2,2,128]{3,2,1,0:T(2,128)S(1)}, f32[1,2,2,128]{3,2,1,0:T(2,128)}, u32[]{:S(2)}) copy-start(f32[1,2,2,128]{3,2,1,0:T(2,128)} %get-tuple-element.40) | copy-start | bytes 6148
  331.9 80.3 %copy-start.43 = (f32[1,2,2,128]{3,2,1,0:T(2,128)S(1)}, f32[1,2,2,128]{3,2,1,0:T(2,128)}, u32[]{:S(2)}) copy-start(f32[1,2,2,128]{3,2,1,0:T(2,128)} %get-tuple-element.38) | copy-start | bytes 6148
  331.9 72.2 %all-to-all-start.1 = ((bf16[2,256,1024]{2,1,0:T(8,128)(2,1)}), bf16[2,256,1024]{2,1,0:T(8,128)(2,1)S(1)}, u32[]{:S(2)}, u32[]{:S(2)}) async-start(bf16[2,256,1024]{2,1,0:T(8,128)(2,1)} %bitcast.210), calls=%async_computation.1 | async-start | bytes 2097152 | tf_op jit(solution)/shard_map/all_to_all | solution.py:166
  408.6 13.8 all-to-all-start.2
  463.2 12.9 all-to-all-start.3
  466.8 59.4 %reduce-scatter.49.cloned.1.call-start = ((), (), s32[]{:S(2)}) async-start(), calls=%async_computation.36 | async-start | bytes 557056
  469.4 132.8 %reduce-scatter.37.cloned.1.call-start = ((), (), s32[]{:S(2)}) async-start(), calls=%async_computation.30 | async-start | bytes 4456448 | tf_op jit(solution)/shard_map/reduce_scatter | solution.py:287
  485.1 192.6 %reduce-scatter.33.cloned.1.call-start = ((), (), s32[]{:S(2)}) async-start(), calls=%async_computation.28 | async-start | bytes 4456448 | tf_op jit(solution)/shard_map/reduce_scatter | solution.py:286
  497.8 255.7 %reduce-scatter.29.cloned.1.call-start = ((), (), s32[]{:S(2)}) async-start(), calls=%async_computation.26 | async-start | bytes 4456448 | tf_op jit(solution)/shard_map/reduce_scatter | solution.py:285
  509.8 319.0 %reduce-scatter.25.cloned.1.call-start = ((), (), s32[]{:S(2)}) async-start(), calls=%async_computation.24 | async-start | bytes 4456448 | tf_op jit(solution)/shard_map/reduce_scatter | solution.py:284
  515.8 361.7 %reduce-scatter.51.cloned.1.call-start = ((), (), s32[]{:S(2)}) async-start(), calls=%async_computation.37 | async-start | bytes 49152
  526.2 373.2 %reduce-scatter.55.cloned.1.call-start = ((), (), s32[]{:S(2)}) async-start(), calls=%async_computation.39 | async-start | bytes 557056
  527.3 430.3 %reduce-scatter.53.cloned.1.call-start = ((), (), s32[]{:S(2)}) async-start(), calls=%async_computation.38 | async-start | bytes 557056
  528.5 510.3 %reduce-scatter.39.cloned.1.call-start = ((), (), s32[]{:S(2)}) async-start(), calls=%async_computation.31 | async-start | bytes 393216 | tf_op jit(solution)/shard_map/reduce_scatter | solution.py:295
  602.2 436.5 %reduce-scatter.35.cloned.1.call-start = ((), (), s32[]{:S(2)}) async-start(), calls=%async_computation.29 | async-start | bytes 393216 | tf_op jit(solution)/shard_map/reduce_scatter | solution.py:294
  677.7 361.1 %reduce-scatter.31.cloned.1.call-start = ((), (), s32[]{:S(2)}) async-start(), calls=%async_computation.27 | async-start | bytes 393216 | tf_op jit(solution)/shard_map/reduce_scatter | solution.py:293
  753.5 285.2 %reduce-scatter.27.cloned.1.call-start = ((), (), s32[]{:S(2)}) async-start(), calls=%async_computation.25 | async-start | bytes 393216 | tf_op jit(solution)/shard_map/reduce_scatter | solution.py:292
  828.9 371.5 %reduce-scatter.45.cloned.1.call-start = ((), (), s32[]{:S(2)}) async-start(), calls=%async_computation.34 | async-start | bytes 17825792 | tf_op jit(solution)/shard_map/reduce_scatter | solution.py:217
  839.4 543.7 %reduce-scatter.43.cloned.1.call-start = ((), (), s32[]{:S(2)}) async-start(), calls=%async_computation.33 | async-start | bytes 17825792 | tf_op jit(solution)/shard_map/reduce_scatter | solution.py:216
  851.0 714.9 %reduce-scatter.41.cloned.1.call-start = ((), (), s32[]{:S(2)}) async-start(), calls=%async_computation.32 | async-start | bytes 17825792 | tf_op jit(solution)/shard_map/reduce_scatter | solution.py:215
  862.6 885.9 %reduce-scatter.47.cloned.1.call-start = ((), (), s32[]{:S(2)}) async-start(), calls=%async_computation.35 | async-start | bytes 17825792 | tf_op jit(solution)/shard_map/reduce_scatter | solution.py:218
  874.3 31.3 %copy-start.19 = (bf16[256,1024]{1,0:T(8,128)(2,1)S(1)}, bf16[256,1024]{1,0:T(8,128)(2,1)}, u32[]{:S(2)}) copy-start(bf16[256,1024]{1,0:T(8,128)(2,1)} %copy-done.18) | copy-start | bytes 1572868
  874.4 31.3 %copy-start.25 = (f32[256,1024]{1,0:T(8,128)S(1)}, f32[256,1024]{1,0:T(8,128)}, u32[]{:S(2)}) copy-start(f32[256,1024]{1,0:T(8,128)} %get-tuple-element.45) | copy-start | bytes 3145732
  (39 other events, 355.9 us)
Sparse Core Ops, SparseCore 0:
  11.1 59.0 all-gather.9
  73.3 55.3 all-gather.7
  131.8 55.3 all-gather.5
  190.2 55.3 all-gather.11
  470.9 55.2 reduce-scatter.48
  530.4 71.7 reduce-scatter.36
  606.0 71.5 reduce-scatter.32
  682.0 71.4 reduce-scatter.28
  757.4 71.4 reduce-scatter.24
  831.0 10.0 reduce-scatter.50
  845.0 54.3 reduce-scatter.54
  902.8 54.8 reduce-scatter.52
  960.6 12.5 reduce-scatter.38
  975.8 11.8 reduce-scatter.34
  990.4 12.0 reduce-scatter.30
  1005.2 11.4 reduce-scatter.26
  1021.8 178.5 reduce-scatter.44
  1205.5 177.5 reduce-scatter.42
  1388.3 177.4 reduce-scatter.40
  1571.0 177.5 reduce-scatter.46
where the time goes:
time: 1760 us
  waiting for transfers between devices  1300 us (74%)
  matrix products  193 us (11%)
  blocking collectives  184 us (10%)
  local copies, waits for them, and re-layouts  25.3 us (1%)
  other arithmetic  24.1 us (1%)
  between operations  17.7 us (1%)
    reduce_scatter x1, waiting for transfers between devices, shards(): lax.psum_scatter(grad_up_one[None], 'grp', scatter_dimension=2, tiled=True)  183 us
    reduce_scatter x1, waiting for transfers between devices, shards(): lax.psum_scatter(grad_down_two[None], 'grp', scatter_dimension=1, tiled=T...  183 us
    reduce_scatter x1, waiting for transfers between devices, shards(): lax.psum_scatter(grad_down_one[None], 'grp', scatter_dimension=1, tiled=T...  183 us
    reduce_scatter x1, waiting for transfers between devices, shards(): lax.psum_scatter(grad_up_two[None], 'grp', scatter_dimension=2, tiled=True)  162 us
    unnamed x24, waiting for transfers between devices  80.4 us
    reduce_scatter x1, waiting for transfers between devices, shards(): lax.psum_scatter(attn_terms[2], 'grp', scatter_dimension=0, tiled=True)  75.8 us
    reduce_scatter x1, waiting for transfers between devices, shards(): lax.psum_scatter(attn_terms[3], 'grp', scatter_dimension=0, tiled=True)  75.4 us
    reduce_scatter x1, waiting for transfers between devices, shards(): lax.psum_scatter(attn_terms[1], 'grp', scatter_dimension=0, tiled=True)  75.3 us
  transfers between devices with their start and end apart: 24, of which 18 were waited for; matrix products, arithmetic and copies ran while one was open for 7% of the time, Pallas kernels for 0%

commit v1 on v0

--- a/solution.py
+++ b/solution.py
@@ -1,6 +1,10 @@
+import functools
+
 import jax
 import jax.numpy as jnp
 from jax import lax
+from jax.experimental import pallas as pl
+from jax.experimental.pallas import tpu as pltpu
 from jax.sharding import PartitionSpec as P
 
 HEADS = 16
@@ -10,6 +14,13 @@
 SQRT_HALF = 0.7071067811865476
 INV_ROOT_TWO_PI = 0.3989422804014327
 HIGH = lax.Precision.HIGHEST
+HALF_LOG2E = -0.7213475204444817
+ERF_P = 0.3275911 * SQRT_HALF
+ERF_A1 = 0.5 * 0.254829592
+ERF_A2 = 0.5 * -0.284496736
+ERF_A3 = 0.5 * 1.421413741
+ERF_A4 = 0.5 * -1.453152027
+ERF_A5 = 0.5 * 1.061405429
 
 
 def norm_parts(rows_in):
@@ -55,6 +66,1091 @@
 
 def fill_slots(rows_in, target, slot_total):
     return jnp.zeros((slot_total, rows_in.shape[1]), rows_in.dtype).at[target].set(rows_in)
+
+
+MESH = pl.DeviceIdType.MESH
+VMEM_CAP = 66 * 1000 * 1000
+
+
+def place(zs):
+    grp = lax.axis_index("grp")
+    ep = lax.axis_index("ep")
+    core = lax.rem(grp, 2)
+    x = lax.rem(lax.div(grp, 2), 2)
+    z = lax.div(grp, 4)
+    return z, x, core, ep
+
+
+def device(z, x, core, ep):
+    return ((z * 2 + x) * 2 + core, ep)
+
+
+def greet(peers):
+    barrier = pltpu.get_barrier_semaphore()
+    for peer in peers:
+        pl.semaphore_signal(barrier, inc=1, device_id=peer, device_id_type=MESH)
+    pl.semaphore_wait(barrier, len(peers))
+
+
+def push(src, dst, send_sem, recv_sem, peer):
+    return pltpu.make_async_remote_copy(
+        src_ref=src, dst_ref=dst, send_sem=send_sem, recv_sem=recv_sem, device_id=peer, device_id_type=MESH
+    )
+
+
+def gather_kernel(zs, *refs):
+    shard = refs[0:5]
+    full = refs[5:10]
+    own_sem, z_send, z_recv, p_send, p_recv, c_send, c_recv = refs[10:]
+    z, x, core, ep = place(zs)
+    right = device(jnp.minimum(z + 1, zs - 1), x, core, ep)
+    left = device(jnp.maximum(z - 1, 0), x, core, ep)
+    x_peer = device(z, 1 - x, core, ep)
+    y_peer = device(z, x, core, 1 - ep)
+    c_peer = device(z, x, 1 - core, ep)
+    others = [device(lax.rem(z + k, zs), x, core, ep) for k in range(1, zs)]
+    half = shard[0].shape[1] // 2
+    items = []
+    for w in range(4):
+        items.append((w, slice(0, half), True))
+        items.append((w, slice(half, 2 * half), False))
+    items.append((4, slice(0, shard[4].shape[1]), True))
+    count = len(items)
+
+    def own(i):
+        w, cols, _ = items[i]
+        return pltpu.make_async_copy(shard[w].at[:, cols], full[w].at[z, x, core, ep, :, cols], own_sem.at[i])
+
+    def z_copy(i, src, slot, way, hop, peer):
+        w, cols, _ = items[i]
+        return push(src, full[w].at[slot, x, core, ep, :, cols], z_send.at[i, way, hop], z_recv.at[i, way, hop], peer)
+
+    def z_start(i):
+        w, cols, _ = items[i]
+
+        @pl.when(z < zs - 1)
+        def _():
+            z_copy(i, shard[w].at[:, cols], z, 0, 0, right).start()
+
+        @pl.when(z > 0)
+        def _():
+            z_copy(i, shard[w].at[:, cols], z, 1, 0, left).start()
+
+    def z_hop(i, hop):
+        w, cols, _ = items[i]
+        low = jnp.maximum(z - hop, 0)
+        high = jnp.minimum(z + hop, zs - 1)
+        from_left = full[w].at[low, x, core, ep, :, cols]
+        from_right = full[w].at[high, x, core, ep, :, cols]
+
+        @pl.when(z >= hop)
+        def _():
+            z_copy(i, from_left, low, 0, hop - 1, right).wait_recv()
+
+        if hop < zs - 1:
+            @pl.when((z >= hop) & (z < zs - 1))
+            def _():
+                z_copy(i, from_left, low, 0, hop, right).start()
+
+        @pl.when(z + hop <= zs - 1)
+        def _():
+            z_copy(i, from_right, high, 1, hop - 1, left).wait_recv()
+
+        if hop < zs - 1:
+            @pl.when((z + hop <= zs - 1) & (z > 0))
+            def _():
+                z_copy(i, from_right, high, 1, hop, left).start()
+
+    def z_drain(i):
+        w, cols, _ = items[i]
+        for hop in range(zs - 1):
+            src = full[w].at[z, x, core, ep, :, cols]
+
+            @pl.when((z < zs - 1) & (z >= hop))
+            def _():
+                z_copy(i, src, z, 0, hop, right).wait_send()
+
+            @pl.when((z > 0) & (z + hop <= zs - 1))
+            def _():
+                z_copy(i, src, z, 1, hop, left).wait_send()
+
+    def second(i):
+        w, cols, x_first = items[i]
+        part = full[w].at[:, x, core, ep, :, cols]
+        return push(part, part, p_send.at[i, 0], p_recv.at[i, 0], x_peer if x_first else y_peer)
+
+    def third(i):
+        w, cols, x_first = items[i]
+        part = full[w].at[:, :, core, ep, :, cols] if x_first else full[w].at[:, x, core, :, :, cols]
+        return push(part, part, p_send.at[i, 1], p_recv.at[i, 1], y_peer if x_first else x_peer)
+
+    def fourth(i):
+        w, cols, _ = items[i]
+        part = full[w].at[:, :, core, :, :, cols]
+        return push(part, part, c_send.at[i], c_recv.at[i], c_peer)
+
+    greet(others + [x_peer, y_peer, c_peer])
+    for i in range(count):
+        z_start(i)
+    for i in range(count):
+        own(i).start()
+    order = [[8, 0, 1], [2, 3], [4, 5], [6, 7]]
+    for t in range(len(order) + 2):
+        if t < len(order):
+            for hop in range(1, zs):
+                for i in order[t]:
+                    z_hop(i, hop)
+            for i in order[t]:
+                own(i).wait()
+                second(i).start()
+        if 1 <= t < len(order) + 1:
+            for i in order[t - 1]:
+                second(i).wait_recv()
+                third(i).start()
+        if t >= 2:
+            for i in order[t - 2]:
+                third(i).wait_recv()
+                fourth(i).start()
+    for i in range(count):
+        fourth(i).wait_recv()
+    for i in range(count):
+        z_drain(i)
+        second(i).wait_send()
+        third(i).wait_send()
+        fourth(i).wait_send()
+
+
+def gather_weights(zs, shards):
+    shapes = [jax.ShapeDtypeStruct((zs, 2, 2, 2) + s.shape, s.dtype) for s in shards]
+    n = 2 * len(shards) - 1
+    dma = pltpu.SemaphoreType.DMA
+    return pl.pallas_call(
+        functools.partial(gather_kernel, zs),
+        out_shape=shapes,
+        in_specs=[pl.BlockSpec(memory_space=pltpu.VMEM)] * len(shards),
+        out_specs=[pl.BlockSpec(memory_space=pl.ANY)] * len(shards),
+        scratch_shapes=[dma((n,)), dma((n, 2, zs)), dma((n, 2, zs)), dma((n, 2)), dma((n, 2)), dma((n,)), dma((n,))],
+        compiler_params=pltpu.CompilerParams(collective_id=1, has_side_effects=True, vmem_limit_bytes=VMEM_CAP),
+        name="gather_weights",
+    )(*shards)
+
+
+def layer_norm(v):
+    center = v - jnp.mean(v, axis=-1, keepdims=True)
+    inverse = lax.rsqrt(jnp.mean(center * center, axis=-1, keepdims=True) + EPSILON)
+    return center * inverse, inverse
+
+
+def gelu_pair(v):
+    tail = jnp.exp2(v * v * HALF_LOG2E)
+    t = 1.0 / (1.0 + ERF_P * jnp.abs(v))
+    poly = ((((ERF_A5 * t + ERF_A4) * t + ERF_A3) * t + ERF_A2) * t + ERF_A1) * t
+    upper = poly * tail
+    phi = jnp.where(v >= 0.0, 1.0 - upper, upper)
+    return v * phi, phi + v * (tail * INV_ROOT_TWO_PI)
+
+
+def expert_forward_kernel(tiles, rows, gain1, gain2, up1, down1, up2, down2, in1, in2, act1, slope1, act2, slope2, middle, delta, sums, acc, sub):
+    layer = pl.program_id(0)
+    t = pl.program_id(1)
+
+    @pl.when((layer == 0) & (t == 0))
+    def _():
+        normed, _ = layer_norm(rows[...].astype(jnp.float32))
+        in1[...] = (normed * gain1[...].astype(jnp.float32)).astype(jnp.bfloat16)
+
+    def step(source, up, down, act, slope):
+        total = source.shape[0]
+        part = total
+
+        def pre_of(i):
+            return jnp.dot(source[i * part : (i + 1) * part], up[0], preferred_element_type=jnp.float32)
+
+        pre = pre_of(0)
+        for i in range(1):
+            nxt = None
+            a, s = gelu_pair(pre)
+            low = a.astype(jnp.bfloat16)
+            act[i * part : (i + 1) * part] = low
+            slope[i * part : (i + 1) * part] = s.astype(jnp.bfloat16)
+            prod = jnp.dot(low, down[0], preferred_element_type=jnp.float32)
+            span = slice(i * part, (i + 1) * part)
+
+            @pl.when(t == 0)
+            def _():
+                acc[span] = prod
+
+            @pl.when(t > 0)
+            def _():
+                acc[span] += prod
+
+            pre = nxt
+
+    @pl.when(layer == 0)
+    def _():
+        step(in1, up1, down1, act1, slope1)
+
+        @pl.when(t == tiles - 1)
+        def _():
+            value = acc[...]
+            sub[...] = value
+            sums[0:1] = jnp.sum(value * value, axis=0, keepdims=True)
+            mid = rows[...].astype(jnp.float32) + value
+            middle[...] = mid
+            normed, _ = layer_norm(mid)
+            in2[...] = (normed * gain2[...].astype(jnp.float32)).astype(jnp.bfloat16)
+
+    @pl.when(layer == 1)
+    def _():
+        step(in2, up2, down2, act2, slope2)
+
+        @pl.when(t == tiles - 1)
+        def _():
+            value = acc[...]
+            sums[1:2] = jnp.sum(value * value, axis=0, keepdims=True)
+            sums[2:8] = jnp.zeros((6, value.shape[1]), jnp.float32)
+            delta[...] = (sub[...] + value).astype(jnp.bfloat16)
+
+
+def expert_forward(rows, gain1, gain2, up1, down1, up2, down2):
+    n, feat = rows.shape
+    hidden = up1.shape[2]
+    tile = 1024
+    tiles = hidden // tile
+    last = tiles - 1
+    bf, f32 = jnp.bfloat16, jnp.float32
+    shape = jax.ShapeDtypeStruct
+    whole = lambda s: pl.BlockSpec(s, lambda l, t: (0,) * len(s))
+    first = lambda l, t: jnp.where(l == 0, t, last)
+    second = lambda l, t: jnp.where(l == 0, 0, t)
+    up = lambda f: pl.BlockSpec((1, feat, tile), lambda l, t: (0, 0, f(l, t)))
+    down = lambda f: pl.BlockSpec((1, tile, feat), lambda l, t: (0, f(l, t), 0))
+    wide = lambda f: pl.BlockSpec((n, tile), lambda l, t: (0, f(l, t)))
+    return pl.pallas_call(
+        functools.partial(expert_forward_kernel, tiles),
+        grid=(2, tiles),
+        in_specs=[whole((n, feat)), whole((1, feat)), whole((1, feat)), up(first), down(first), up(second), down(second)],
+        out_specs=[whole((n, feat))] * 2 + [wide(first)] * 2 + [wide(second)] * 2 + [whole((n, feat))] * 2 + [whole((8, feat))],
+        out_shape=[shape((n, feat), bf)] * 2 + [shape((n, hidden), bf)] * 4 + [shape((n, feat), f32), shape((n, feat), bf), shape((8, feat), f32)],
+        scratch_shapes=[pltpu.VMEM((n, feat), f32), pltpu.VMEM((n, feat), f32)],
+        compiler_params=pltpu.CompilerParams(vmem_limit_bytes=VMEM_CAP, dimension_semantics=("arbitrary", "arbitrary")),
+        name="expert_forward",
+    )(rows, gain1, gain2, up1, down1, up2, down2)
+
+
+def attend_kernel(heads, x, gain, wq, wk, wv, wo, cents, routes, prefix, cotangent, attn_in, queries, keys, values, context, hidden, gate, pick, slot_rows, slot_grads, sums, ctx):
+    bf, f32 = jnp.bfloat16, jnp.float32
+    tokens, feat = x.shape
+    pair = 2 * feat // heads
+    scale = (feat // heads) ** -0.5
+    wide = x[...].astype(f32)
+    normed, _ = layer_norm(wide)
+    attn_in[...] = (normed * gain[...].astype(f32)).astype(bf)
+    for w, out in ((wq, queries), (wk, keys), (wv, values)):
+        out[...] = jnp.dot(attn_in[...], w[...], preferred_element_type=f32).astype(bf)
+    row_ids = lax.broadcasted_iota(jnp.int32, (tokens, tokens), 0)
+    col_ids = lax.broadcasted_iota(jnp.int32, (tokens, tokens), 1)
+    visible = (col_ids <= row_ids) | (col_ids < prefix[0])
+    low_half = lax.broadcasted_iota(jnp.int32, (tokens, pair), 1) < pair // 2
+    last_dims = (((1,), (1,)), ((), ()))
+
+    def body(h, carry):
+        cols = pl.ds(pl.multiple_of(h * pair, pair), pair)
+        q, k, v = queries[:, cols], keys[:, cols], values[:, cols]
+        outs = []
+        for side in (low_half, jnp.logical_not(low_half)):
+            mine = jnp.where(side, q, jnp.zeros_like(q))
+            s = lax.dot_general(mine, k, last_dims, preferred_element_type=f32) * scale
+            s = jnp.where(visible, s, -1e30)
+            top = jnp.max(s, axis=-1, keepdims=True)
+            total = top + jnp.log(jnp.sum(jnp.exp(s - top), axis=-1, keepdims=True))
+            p = jnp.exp(s - total).astype(bf)
+            outs.append(jnp.dot(p, v, preferred_element_type=f32))
+        ctx[:, cols] = jnp.where(low_half, outs[0], outs[1]).astype(bf)
+        return carry
+
+    lax.fori_loop(0, heads // 2, body, 0)
+    context[...] = ctx[...]
+    branch = jnp.dot(ctx[...], wo[...], preferred_element_type=f32)
+    sums[...] = jnp.broadcast_to(jnp.sum(branch * branch, axis=0, keepdims=True), sums.shape)
+    hid = wide + branch
+    hidden[...] = hid
+    low = hid.astype(bf)
+    scores = lax.dot_general(low, cents[...], last_dims, preferred_element_type=f32)
+    lane = lax.broadcasted_iota(jnp.int32, scores.shape, 1)
+    hot = (lane == routes[...]).astype(f32)
+    g = 1.0 / (1.0 + jnp.exp(-jnp.sum(scores * hot, axis=1, keepdims=True)))
+    gate[...] = g
+    tri = (col_ids <= row_ids).astype(bf)
+    count = jnp.dot(tri, hot.astype(bf), preferred_element_type=f32)
+    position = jnp.sum(count * hot, axis=1, keepdims=True) - 1.0
+    target = routes[...] * tokens + position.astype(jnp.int32)
+    slots = lax.broadcasted_iota(jnp.int32, (tokens, 2 * tokens), 1)
+    chosen = (slots == target).astype(bf)
+    pick[...] = chosen
+    first_dims = (((0,), (0,)), ((), ()))
+    slot_rows[...] = lax.dot_general(chosen, low, first_dims, preferred_element_type=f32).astype(bf)
+    grads = (g * cotangent[...].astype(f32)).astype(bf)
+    slot_grads[...] = lax.dot_general(chosen, grads, first_dims, preferred_element_type=f32).astype(bf)
+
+
+def attend(heads, x, gain, wq, wk, wv, wo, cents, routes, prefix, cotangent):
+    tokens, feat = x.shape
+    bf, f32 = jnp.bfloat16, jnp.float32
+    shape = jax.ShapeDtypeStruct
+    vm = pl.BlockSpec(memory_space=pltpu.VMEM)
+    return pl.pallas_call(
+        functools.partial(attend_kernel, heads),
+        in_specs=[vm] * 8 + [pl.BlockSpec(memory_space=pltpu.SMEM), vm],
+        out_specs=[vm] * 11,
+        out_shape=[shape((tokens, feat), bf)] * 5
+        + [shape((tokens, feat), f32), shape((tokens, 1), f32), shape((tokens, 2 * tokens), bf)]
+        + [shape((2 * tokens, feat), bf)] * 2
+        + [shape((8, feat), f32)],
+        scratch_shapes=[pltpu.VMEM((tokens, feat), bf)],
+        compiler_params=pltpu.CompilerParams(vmem_limit_bytes=VMEM_CAP),
+        name="attend",
+    )(x, gain, wq, wk, wv, wo, cents, routes, prefix, cotangent)
+
+
+SLICES = 4
+LEAD = 2
+RING = 8
+
+
+def step_kernel(zs, heads, *refs):
+    (x_ref, attn_in_ref, q_ref, k_ref, v_ref, context_ref, cot_ref, hidden_ref, pick_ref, wq, wk, wv, wo) = refs[0:13]
+    (act_one, act_two, slope_one, slope_two, in_one, in_two, grads, rows_ref, delta, middle, up1, down1, up2, down2) = refs[13:27]
+    gain, cents, gain1, gain2, gate, routes, branch_sq, sub_sq, prefix = refs[27:36]
+    out_w = refs[36]
+    out_a = refs[37:41]
+    small_grp, small_all, result, input_grad = refs[41:45]
+    pre_two, pre_one, sub_grad, row_grad, wide_far, narrow_far, attn_far, back_far, grad_far = refs[45:54]
+    (send, xrecv, zrecv, acc, tiles, sides, prod, ep_in, x_in, z_in, small_in, small_ref) = refs[54:66]
+    (wd, wu, sl, ps, hb, accf, midf, loadf, picks) = refs[66:75]
+    (wf_s, wf_r, nf_s, nf_r, xs, xr, zsem_s, zsem_r, es, er, axs, axr, azs, azr, ss, sr, tile_sem, side_sem) = refs[75:93]
+    (af_s, af_r, y_s, y_r, w_sem, ps_sem, ld_sem, out_sem) = refs[93:]
+    wide = (act_two, pre_two, act_one, pre_one)
+    narrow = (grads, in_two, sub_grad, in_one)
+    bf, f32 = jnp.bfloat16, jnp.float32
+    z, x, core, ep = place(zs)
+    tokens, feat = x_ref.shape
+    rows = 2 * tokens
+    hidden = act_one.shape[1]
+    chunk = out_w.shape[1]
+    per = prod.shape[4]
+    blocks = 4 * zs
+    size = chunk // SLICES
+    right = device(jnp.minimum(z + 1, zs - 1), x, core, ep)
+    left = device(jnp.maximum(z - 1, 0), x, core, ep)
+    x_peer = device(z, 1 - x, core, ep)
+    y_peer = device(z, x, core, 1 - ep)
+    c_peer = device(z, x, 1 - core, ep)
+    others = [device(lax.rem(z + k, zs), x, core, ep) for k in range(1, zs)]
+    contract0 = (((0,), (0,)), ((), ()))
+    last_dims = (((1,), (1,)), ((), ()))
+
+    def dest(k):
+        to_right = zs - 1 - z
+        d = jnp.where(k < to_right, zs - 1 - k, k - to_right)
+        return jnp.where(k < zs - 1, d, z)
+
+    def begins(d):
+        return ((d > z) & (z == 0)) | ((d < z) & (z == zs - 1))
+
+    def fetch(pairs):
+        copies = [pltpu.make_async_copy(src, dst, ld_sem.at[i]) for i, (src, dst) in enumerate(pairs)]
+        for c in copies:
+            c.start()
+        for c in copies:
+            c.wait()
+
+    def two(slot):
+        return hb.at[pl.ds(slot, 2)]
+
+    def flat(slot):
+        return hb[pl.ds(slot, 2)].reshape(rows, feat)
+
+    greet(others + [x_peer, y_peer, c_peer])
+
+    def far_wide(w, q):
+        j = q * 2 + (1 - core)
+        return push(
+            wide[w].at[:, pl.ds(pl.multiple_of(j * chunk, chunk), chunk)], wide_far.at[w, q], wf_s.at[w], wf_r.at[w], c_peer
+        )
+
+    def far_narrow(w):
+        return push(narrow[w], narrow_far.at[w], nf_s.at[w], nf_r.at[w], c_peer)
+
+    def all_far(w):
+        return push(wide_far.at[w], wide_far.at[w], wf_s.at[w], wf_r.at[w], c_peer)
+
+    def send_wide(w):
+        def send_far(q, carry):
+            far_wide(w, q).start()
+            return carry
+
+        lax.fori_loop(0, 2 * zs, send_far, 0)
+
+    def far_attn(i, src):
+        return push(src, attn_far.at[i], af_s.at[i], af_r.at[i], c_peer)
+
+    def far_delta():
+        return push(delta.at[1 - ep], back_far, y_s.at[0], y_r.at[0], y_peer)
+
+    def far_rows():
+        return push(row_grad.at[1 - ep], grad_far, y_s.at[1], y_r.at[1], y_peer)
+
+    far_narrow(0).start()
+    send_wide(0)
+    far_delta().start()
+    far_narrow(1).start()
+    far_narrow(3).start()
+    far_attn(0, attn_in_ref).start()
+    far_attn(1, context_ref).start()
+
+    def load_tile(w, q, slot):
+        j = q * 2 + core
+        for i in range(4):
+            @pl.when(w == i)
+            def _():
+                pltpu.make_async_copy(
+                    wide[i].at[:, pl.ds(pl.multiple_of(j * chunk, chunk), chunk)],
+                    tiles.at[slot, pl.ds(0, rows), :],
+                    tile_sem.at[slot, 0],
+                ).start()
+
+        pltpu.make_async_copy(wide_far.at[w, q], tiles.at[slot, pl.ds(rows, rows), :], tile_sem.at[slot, 1]).start()
+
+    def wait_tile(slot):
+        for i in range(2):
+            part = tiles.at[slot, pl.ds(i * rows, rows), :]
+            pltpu.make_async_copy(part, part, tile_sem.at[slot, i]).wait()
+
+    def load_side(w):
+        slot = lax.rem(w, 2)
+        for i in range(4):
+            @pl.when(w == i)
+            def _():
+                pltpu.make_async_copy(narrow[i], sides.at[slot, pl.ds(0, 2)], side_sem.at[0]).start()
+
+        pltpu.make_async_copy(narrow_far.at[w], sides.at[slot, pl.ds(2, 2)], side_sem.at[1]).start()
+
+    def wait_side(w):
+        slot = lax.rem(w, 2)
+        for i in range(2):
+            part = sides.at[slot, pl.ds(2 * i, 2)]
+            pltpu.make_async_copy(part, part, side_sem.at[i]).wait()
+
+    def product(w, slot):
+        side = sides[lax.rem(w, 2)].reshape(2 * rows, feat)
+        return lax.dot_general(tiles[slot], side, contract0, preferred_element_type=f32)
+
+    def span(s):
+        return pl.ds(pl.multiple_of(s * size, size), size)
+
+    def x_copy(b, s):
+        return push(send.at[lax.rem(b, RING), span(s), :], xrecv.at[b, span(s), :], xs.at[b, s], xr.at[b, s], x_peer)
+
+    def z_copy(b, s):
+        w = lax.div(b, zs)
+        d = dest(lax.rem(b, zs))
+        to_right = d > z
+        nxt = jnp.where(to_right, z + 1, z - 1)
+        slot = jnp.where(d != nxt, d, jnp.where(to_right, d, zs))
+        return push(
+            send.at[lax.rem(b, RING), span(s), :], zrecv.at[w, slot, span(s), :], zsem_s.at[b, s],
+            zsem_r.at[w, slot, s], device(nxt, x, core, ep),
+        )
+
+    def z_wait(w, slot, s):
+        ref = zrecv.at[w, slot, span(s), :]
+        push(ref, ref, zsem_s.at[0, s], zsem_r.at[w, slot, s], x_peer).wait_recv()
+        return ref[...].astype(f32)
+
+    def z_sent(b):
+        @pl.when(lax.rem(b, zs) < zs - 1)
+        def _():
+            for s in range(SLICES):
+                z_copy(b, s).wait_send()
+
+    def q_first(b):
+        return dest(lax.rem(b, zs)) * 2 + (1 - x)
+
+    def q_second(b):
+        return dest(lax.rem(b, zs)) * 2 + x
+
+    def far_wait(w):
+        for i in range(4):
+            @pl.when(w == i)
+            def _():
+                far_narrow(i).wait_recv()
+                all_far(i).wait_recv()
+
+    def stage_one(b):
+        w = lax.div(b, zs)
+        slot = lax.rem(b, 2)
+
+        @pl.when(lax.rem(b, zs) == 0)
+        def _():
+            far_wait(w)
+            load_side(w)
+            load_tile(w, q_first(b), slot)
+            wait_side(w)
+
+        wait_tile(slot)
+
+        @pl.when(lax.rem(b, zs) < zs - 1)
+        def _():
+            load_tile(w, q_first(b + 1), 1 - slot)
+
+        @pl.when(b >= RING)
+        def _():
+            z_sent(b - RING)
+
+        send[lax.rem(b, RING)] = product(w, slot).astype(bf)
+
+    def stage_two(b):
+        w = lax.div(b, zs)
+        d = dest(lax.rem(b, zs))
+        slot = 2 + lax.rem(b, 2)
+        mine = lax.rem(b, RING)
+        wait_tile(slot)
+
+        @pl.when(b + 1 < blocks)
+        def _():
+            load_tile(lax.div(b + 1, zs), q_second(b + 1), 5 - slot)
+
+        acc[...] = product(w, slot)
+
+        def piece(s, carry):
+            sp = span(s)
+            x_copy(b, s).wait()
+            acc[sp, :] += xrecv[b, sp, :].astype(f32)
+
+            @pl.when(d != z)
+            def _():
+                @pl.when(jnp.logical_not(begins(d)))
+                def _():
+                    acc[sp, :] += z_wait(w, d, s)
+
+                send[mine, sp, :] = acc[sp, :].astype(bf)
+
+                @pl.when(s > 0)
+                def _():
+                    z_copy(b, s - 1).start()
+
+            @pl.when(d == z)
+            def _():
+                acc[sp, :] += z_wait(w, jnp.where(z > 0, z, zs), s)
+
+                @pl.when((z > 0) & (z < zs - 1))
+                def _():
+                    acc[sp, :] += z_wait(w, zs, s)
+
+            return carry
+
+        lax.fori_loop(0, SLICES, piece, 0)
+
+        @pl.when(d != z)
+        def _():
+            z_copy(b, SLICES - 1).start()
+
+        @pl.when(d == z)
+        def _():
+            copy = pltpu.make_async_copy(acc, out_w.at[w], out_sem)
+            copy.start()
+            copy.wait()
+
+    tile = wd.shape[1]
+
+    def stream(source, start, count, up, down, slope, pre):
+        def copies(t, slot):
+            cols = pl.ds(pl.multiple_of(t * tile, tile), tile)
+            return (
+                pltpu.make_async_copy(down.at[0, cols, :], wd.at[slot], w_sem.at[slot, 0]),
+                pltpu.make_async_copy(up.at[0, :, cols], wu.at[slot], w_sem.at[slot, 1]),
+                pltpu.make_async_copy(slope.at[pl.ds(start, count), cols], sl.at[slot, pl.ds(0, count), :], w_sem.at[slot, 2]),
+            )
+
+        def out(t, slot):
+            cols = pl.ds(pl.multiple_of(t * tile, tile), tile)
+            return pltpu.make_async_copy(ps.at[slot, pl.ds(0, count), :], pre.at[pl.ds(start, count), cols], ps_sem.at[slot])
+
+        steps = hidden // tile
+        for c in copies(0, 0):
+            c.start()
+
+        def body(t, carry):
+            slot = lax.rem(t, 2)
+            for c in copies(t, slot):
+                c.wait()
+
+            @pl.when(t + 1 < steps)
+            def _():
+                for c in copies(t + 1, 1 - slot):
+                    c.start()
+
+            g = lax.dot_general(source(), wd[slot], last_dims, preferred_element_type=f32)
+            low = (g * sl[slot, 0:count].astype(f32)).astype(bf)
+
+            @pl.when(t >= 2)
+            def _():
+                out(t - 2, slot).wait()
+
+            ps[slot, 0:count] = low
+            out(t, slot).start()
+            value = lax.dot_general(low, wu[slot], last_dims, preferred_element_type=f32)
+
+            @pl.when(t == 0)
+            def _():
+                accf[0:count] = value
+
+            @pl.when(t > 0)
+            def _():
+                accf[0:count] += value
+
+            return carry
+
+        lax.fori_loop(0, steps, body, 0)
+        out(steps - 2, lax.rem(steps - 2, 2)).wait()
+        out(steps - 1, lax.rem(steps - 1, 2)).wait()
+
+    part = 64
+
+    def norm_parts_of(value, g, gain_row):
+        normed, inverse = layer_norm(value)
+        total = jnp.sum(g * normed, axis=0, keepdims=True)
+        q = g * gain_row
+        mean_q = jnp.mean(q, axis=-1, keepdims=True)
+        mean_dot = jnp.mean(q * normed, axis=-1, keepdims=True)
+        return total, inverse * (q - mean_q - normed * mean_dot)
+
+    def event_second():
+        fetch([(grads, two(0)), (middle, loadf), (rows_ref, two(2))])
+        stream(lambda: flat(0), 0, rows, up2, down2, slope_two, pre_two)
+        send_wide(1)
+        small_ref[...] = jnp.zeros_like(small_ref)
+        gain_row = gain2[...].astype(f32)
+        per_block = tokens // part
+
+        def body(i, carry):
+            at = pl.ds(pl.multiple_of(i * part, part), part)
+            total, value = norm_parts_of(loadf[at], accf[at], gain_row)
+            small_ref[1:2] += total
+            midf[at] = value
+            blk = lax.div(i, per_block)
+            sub = pl.ds(pl.multiple_of(lax.rem(i, per_block) * part, part), part)
+            hb[4 + blk, sub] = (hb[blk, sub].astype(f32) + value).astype(bf)
+            return carry
+
+        lax.fori_loop(0, rows // part, body, 0)
+        fetch([(two(4), sub_grad)])
+        far_narrow(2).start()
+        send_wide(2)
+
+    def event_first(blk):
+        start = pl.multiple_of(blk * tokens, tokens)
+        stream(lambda: hb[4 + blk], start, tokens, up1, down1, slope_one, pre_one)
+        gain_row = gain1[...].astype(f32)
+
+        def body(i, carry):
+            at = pl.ds(pl.multiple_of(i * part, part), part)
+            value = hb[2 + blk, at].astype(f32)
+            total, back = norm_parts_of(value, accf[at], gain_row)
+            small_ref[0:1] += total
+            mid = midf[pl.ds(pl.multiple_of(blk * tokens + i * part, part), part)]
+            hb[6 + blk, at] = (back + mid).astype(bf)
+            return carry
+
+        lax.fori_loop(0, tokens // part, body, 0)
+        fetch([(hb.at[6 + blk], row_grad.at[blk])])
+
+    def event_first_far():
+        event_first(1 - ep)
+        far_rows().start()
+
+    def event_first_own():
+        event_first(ep)
+        send_wide(3)
+
+    def event_attend():
+        far_delta().wait_recv()
+        far_rows().wait_recv()
+        fetch(
+            [
+                (cot_ref, hb.at[1]),
+                (delta.at[ep], hb.at[3]),
+                (back_far, hb.at[5]),
+                (row_grad.at[ep], hb.at[7]),
+                (grad_far, hb.at[9]),
+                (q_ref, hb.at[12]),
+                (k_ref, hb.at[13]),
+                (v_ref, hb.at[14]),
+                (x_ref, hb.at[11]),
+                (attn_in_ref, hb.at[0]),
+                (context_ref, hb.at[2]),
+                (hidden_ref, loadf.at[pl.ds(0, tokens)]),
+                (pick_ref, picks),
+                (wo.at[pl.ds(0, feat // 2)], wd.at[0]),
+                (wo.at[pl.ds(feat // 2, feat // 2)], wd.at[1]),
+            ]
+        )
+        c = cents[...].astype(f32)
+
+        def combine(i, carry):
+            at = pl.ds(pl.multiple_of(i * part, part), part)
+            own = picks[at, pl.ds(pl.multiple_of(ep * tokens, tokens), tokens)]
+            far = picks[at, pl.ds(pl.multiple_of((1 - ep) * tokens, tokens), tokens)]
+            returned = jnp.dot(own, hb[3], preferred_element_type=f32) + jnp.dot(far, hb[5], preferred_element_type=f32)
+            back = jnp.dot(own, hb[7], preferred_element_type=f32) + jnp.dot(far, hb[9], preferred_element_type=f32)
+            g = gate[at]
+            hid = loadf[at]
+            res = hid + g * returned
+            hb[15, at] = res.astype(bf)
+            small_ref[5:6] += jnp.sum(res * res, axis=0, keepdims=True)
+            grad_out = hb[1, at].astype(f32)
+            grad_score = jnp.sum(grad_out * returned, axis=1, keepdims=True) * g * (1.0 - g)
+            is_first = routes[at] == 0
+            weighted = grad_score * hid.astype(bf).astype(f32)
+            zero = jnp.zeros_like(weighted)
+            small_ref[3:4] += jnp.sum(jnp.where(is_first, weighted, zero), axis=0, keepdims=True)
+            small_ref[4:5] += jnp.sum(jnp.where(is_first, zero, weighted), axis=0, keepdims=True)
+            grad_hidden = grad_out + grad_score * jnp.where(is_first, c[0:1], c[1:2]) + back
+            midf[at] = grad_hidden
+            hb[10, at] = grad_hidden.astype(bf)
+            return carry
+
+        lax.fori_loop(0, tokens // part, combine, 0)
+        fetch([(hb.at[15], result)])
+        half = feat // 2
+        for i in range(2):
+            hb[15, :, i * half : (i + 1) * half] = lax.dot_general(
+                hb[10], wd[i], last_dims, preferred_element_type=f32
+            ).astype(bf)
+        row_ids = lax.broadcasted_iota(jnp.int32, (tokens, tokens), 0)
+        col_ids = lax.broadcasted_iota(jnp.int32, (tokens, tokens), 1)
+        pair = 2 * feat // heads
+        scale = (feat // heads) ** -0.5
+        limit = prefix[...]
+
+        def head(h, carry):
+            visible = (col_ids <= row_ids) | (col_ids < limit)
+            low_half = lax.broadcasted_iota(jnp.int32, (tokens, pair), 1) < pair // 2
+            cols = pl.ds(pl.multiple_of(h * pair, pair), pair)
+            q, k, v, gc = hb[12, :, cols], hb[13, :, cols], hb[14, :, cols], hb[15, :, cols]
+            outs = []
+            for side in (low_half, jnp.logical_not(low_half)):
+                s = lax.dot_general(jnp.where(side, q, jnp.zeros_like(q)), k, last_dims, preferred_element_type=f32) * scale
+                s = jnp.where(visible, s, -1e30)
+                top = jnp.max(s, axis=-1, keepdims=True)
+                total = top + jnp.log(jnp.sum(jnp.exp(s - top), axis=-1, keepdims=True))
+                p = jnp.exp(s - total)
+                gp = lax.dot_general(jnp.where(side, gc, jnp.zeros_like(gc)), v, last_dims, preferred_element_type=f32)
+                dot = jnp.sum(gp * p, axis=-1, keepdims=True)
+                gs = (p * (gp - dot)).astype(bf)
+                outs.append(
+                    (
+                        jnp.dot(gs, k, preferred_element_type=f32),
+                        lax.dot_general(gs, q, contract0, preferred_element_type=f32),
+                        lax.dot_general(p.astype(bf), gc, contract0, preferred_element_type=f32),
+                    )
+                )
+            hb[4, :, cols] = (jnp.where(low_half, outs[0][0], outs[1][0]) * scale).astype(bf)
+            hb[6, :, cols] = (jnp.where(low_half, outs[0][1], outs[1][1]) * scale).astype(bf)
+            hb[8, :, cols] = jnp.where(low_half, outs[0][2], outs[1][2]).astype(bf)
+            return carry
+
+        lax.fori_loop(0, heads // 2, head, 0)
+        loads = [(m, i) for i in range(2) for m in (wq, wk, wv)]
+
+        def weight_copy(n):
+            m, i = loads[n]
+            return pltpu.make_async_copy(m.at[pl.ds(i * half, half)], wd.at[n % 2], w_sem.at[n % 2, 0])
+
+        weight_copy(0).start()
+        for n in range(6):
+            weight_copy(n).wait()
+            if n < 5:
+                weight_copy(n + 1).start()
+            value = lax.dot_general(hb[4 + 2 * (n % 3)], wd[n % 2], last_dims, preferred_element_type=f32)
+            cols = slice((n // 3) * half, (n // 3 + 1) * half)
+            if n % 3 == 0:
+                accf[0:tokens, cols] = value
+            else:
+                accf[0:tokens, cols] += value
+        for i in range(4):
+            far_attn(2 + i, hb.at[4 + 2 * i]).start()
+        gain_row = gain[...].astype(f32)
+
+        def norms(i, carry):
+            at = pl.ds(pl.multiple_of(i * part, part), part)
+            total, value = norm_parts_of(hb[11, at].astype(f32), accf[at], gain_row)
+            small_ref[2:3] += total
+            midf[at] += value
+            return carry
+
+        lax.fori_loop(0, tokens // part, norms, 0)
+        small_ref[6:7] = branch_sq[0:1]
+        small_ref[7:9] = sub_sq[0:2]
+        start0()
+        for i in range(6):
+            far_attn(i, hb.at[0]).wait_recv()
+        fetch(
+            [(midf.at[pl.ds(0, tokens)], input_grad)]
+            + [(attn_far.at[i], hb.at[2 * i + 1]) for i in range(6)]
+        )
+        step = 8 * per
+
+        for w in range(4):
+            lhs = 0 if w < 3 else 2
+            rhs = 4 + 2 * w
+
+            def form(m, carry):
+                cols = pl.ds(pl.multiple_of(m * step, step), step)
+                left_part = hb[pl.ds(lhs, 2), :, cols].reshape(rows, step)
+                value = lax.dot_general(left_part, flat(rhs), contract0, preferred_element_type=f32)
+                value = value.astype(bf).reshape(2, 2, 2 * per, feat)
+                mine = jnp.where(core == 0, value[:, 0], value[:, 1])
+                prod[w, m] = mine.reshape(2, 2, per, feat)
+                return carry
+
+            lax.fori_loop(0, zs, form, 0)
+            if w > 0:
+                attn_ep(w - 1).start()
+        for i in range(6):
+            far_attn(i, hb.at[0]).wait_send()
+        attn_ep(3).start()
+
+    def attn_ep(w):
+        return push(prod.at[w, :, :, 1 - ep], ep_in.at[w], es.at[w], er.at[w], y_peer)
+
+    def attn_x(w):
+        return push(prod.at[w, :, 1 - x, ep], x_in.at[w], axs.at[w], axr.at[w], x_peer)
+
+    def fold_ep(w):
+        attn_ep(w).wait()
+
+        def body(m, carry):
+            for i in range(2):
+                total = prod[w, m, i, ep].astype(f32) + ep_in[w, m, i].astype(f32)
+                prod[w, m, i, ep] = total.astype(bf)
+            return carry
+
+        lax.fori_loop(0, zs, body, 0)
+
+    def attn_z_copy(w, k):
+        d = dest(k)
+        to_right = d > z
+        nxt = jnp.where(to_right, z + 1, z - 1)
+        slot = jnp.where(d != nxt, d, jnp.where(to_right, d, zs))
+        return push(prod.at[w, d, x, ep], z_in.at[w, slot], azs.at[w, k], azr.at[w, slot], device(nxt, x, core, ep))
+
+    def attn_z_wait(w, slot):
+        ref = z_in.at[w, slot]
+        push(ref, ref, azs.at[w, 0], azr.at[w, slot], x_peer).wait_recv()
+        return ref[...].astype(f32)
+
+    def fold_x(w):
+        attn_x(w).wait()
+
+        def body(k, carry):
+            d = dest(k)
+            total = prod[w, d, x, ep].astype(f32) + x_in[w, d].astype(f32)
+            prod[w, d, x, ep] = total.astype(bf)
+            return carry
+
+        lax.fori_loop(0, zs, body, 0)
+
+    def fold_z(w):
+        def body(k, carry):
+            d = dest(k)
+
+            @pl.when(jnp.logical_not(begins(d)))
+            def _():
+                total = prod[w, d, x, ep].astype(f32) + attn_z_wait(w, d)
+                prod[w, d, x, ep] = total.astype(bf)
+
+            attn_z_copy(w, k).start()
+            return carry
+
+        lax.fori_loop(0, zs - 1, body, 0)
+
+    def last_z(w):
+        first = jnp.where(z > 0, z, zs)
+        out_a[w][...] = prod[w, z, x, ep].astype(f32) + attn_z_wait(w, first)
+
+        @pl.when((z > 0) & (z < zs - 1))
+        def _():
+            out_a[w][...] += attn_z_wait(w, zs)
+
+        for k in range(zs - 1):
+            attn_z_copy(w, k).wait_send()
+
+    def small_stage(stage, n, mine, peer_at, src):
+        def copy(k):
+            return push(src, small_in.at[stage, mine], ss.at[stage, k], sr.at[stage, k], peer_at(lax.rem(mine + k, n)))
+
+        def start():
+            for k in range(1, n):
+                copy(k).start()
+
+        def end():
+            for k in range(1, n):
+                copy(k).wait()
+            small_in[stage, mine] = src[...]
+            total = small_in[stage, 0]
+            for i in range(1, n):
+                total = total + small_in[stage, i]
+            return total
+
+        return start, end
+
+    start0, end0 = small_stage(0, 2, core, lambda i: device(z, x, i, ep), small_ref)
+    start1, end1 = small_stage(1, 2, x, lambda i: device(z, i, core, ep), small_in.at[3, 3])
+    start2, end2 = small_stage(2, zs, z, lambda i: device(i, x, core, ep), small_in.at[3, 2])
+    start3, end3 = small_stage(3, 2, ep, lambda i: device(z, x, core, i), small_grp)
+
+    def event_x(w):
+        def act():
+            fold_ep(w)
+            attn_x(w).start()
+
+        return act
+
+    def event_small1():
+        small_in[3, 3] = end0()
+        start1()
+
+    def event_small2():
+        small_in[3, 2] = end1()
+        start2()
+
+    def event_small3():
+        small_grp[...] = end2()
+        start3()
+
+    def event_z(w):
+        def act():
+            fold_x(w)
+            fold_z(w)
+
+        return act
+
+    def event_last():
+        for w in range(4):
+            last_z(w)
+        small_all[...] = end3()
+
+    events = EVENTS(
+        event_second, event_first_far, event_first_own, event_attend, event_x, event_small1, event_small2, event_small3,
+        event_z, event_last,
+    )
+
+    def pipeline(t, carry):
+        for at, action in events:
+            pl.when(t == at)(action)
+
+        @pl.when(t < blocks)
+        def _():
+            stage_one(t)
+
+        @pl.when((t > 0) & (t <= blocks))
+        def _():
+            for s in range(SLICES):
+                x_copy(t - 1, s).start()
+
+        @pl.when(t == LEAD - 1)
+        def _():
+            load_tile(0, q_second(0), 2)
+
+        @pl.when(t >= LEAD)
+        def _():
+            stage_two(t - LEAD)
+
+        return carry
+
+    lax.fori_loop(0, blocks + LEAD, pipeline, 0)
+    event_last()
+
+    def drain(b, carry):
+        z_sent(b)
+        return carry
+
+    lax.fori_loop(blocks - RING, blocks, drain, 0)
+    for w in range(4):
+        far_narrow(w).wait_send()
+        all_far(w).wait_send()
+    far_delta().wait_send()
+    far_rows().wait_send()
+
+
+def EVENTS(second, first_far, first_own, attend_event, x_of, small1, small2, small3, z_of, last):
+    found = [(2, second), (5, first_far), (7, first_own), (9, attend_event)]
+    found += [(11, small1), (12, small2), (13, small3)]
+    found += [(11 + w, x_of(w)) for w in range(4)]
+    found += [(14 + w, z_of(w)) for w in range(4)]
+    return found
+
+
+def backward_step(zs, heads, big, experts, little, prefix):
+    x, hidden = big[0], experts[0].shape[1]
+    tokens, feat = x.shape
+    rows = 2 * tokens
+    chunk = hidden // (4 * zs)
+    per = feat // (8 * zs)
+    f32, bf = jnp.float32, jnp.bfloat16
+    shape = jax.ShapeDtypeStruct
+    vm = pl.BlockSpec(memory_space=pltpu.VMEM)
+    hbm = pl.BlockSpec(memory_space=pl.ANY)
+    dma = pltpu.SemaphoreType.DMA
+    outs = [shape((4, chunk, feat), f32)]
+    outs += [shape((per, feat), f32)] * 4
+    outs += [shape((16, feat), f32)] * 2
+    outs += [shape((tokens, feat), bf), shape((tokens, feat), f32)]
+    outs += [shape((rows, hidden), bf)] * 2 + [shape((2, tokens, feat), bf)] * 2
+    outs += [shape((4, 2 * zs, rows, chunk), bf), shape((4, 2, tokens, feat), bf), shape((6, tokens, feat), bf)]
+    outs += [shape((tokens, feat), bf)] * 2
+    s = SLICES
+    blocks = 4 * zs
+    tile = 512
+    vmem = pltpu.VMEM
+    return pl.pallas_call(
+        functools.partial(step_kernel, zs, heads),
+        out_shape=outs,
+        in_specs=[hbm] * 27 + [vm] * 9,
+        out_specs=[hbm] + [vm] * 6 + [hbm] * 11,
+        scratch_shapes=[
+            vmem((RING, chunk, feat), bf),
+            vmem((blocks, chunk, feat), bf),
+            vmem((4, zs + 1, chunk, feat), bf),
+            vmem((chunk, feat), f32),
+            vmem((4, 2 * rows, chunk), bf),
+            vmem((2, 4, tokens, feat), bf),
+            vmem((4, zs, 2, 2, per, feat), bf),
+            vmem((4, zs, 2, per, feat), bf),
+            vmem((4, zs, per, feat), bf),
+            vmem((4, zs + 1, per, feat), bf),
+            vmem((4, max(zs, 4), 16, feat), f32),
+            vmem((16, feat), f32),
+            vmem((2, tile, feat), bf),
+            vmem((2, feat, tile), bf),
+            vmem((2, rows, tile), bf),
+            vmem((2, rows, tile), bf),
+            vmem((16, tokens, feat), bf),
+            vmem((rows, feat), f32),
+            vmem((rows, feat), f32),
+            vmem((rows, feat), f32),
+            vmem((tokens, rows), bf),
+            dma((4,)), dma((4,)), dma((4,)), dma((4,)),
+            dma((blocks, s)), dma((blocks, s)), dma((blocks, s)), dma((4, zs + 1, s)),
+            dma((4,)), dma((4,)), dma((4,)), dma((4,)), dma((4, zs)), dma((4, zs + 1)),
+            dma((4, zs)), dma((4, zs)), dma((4, 2)), dma((2,)),
+            dma((6,)), dma((6,)), dma((2,)), dma((2,)), dma((2, 3)), dma((2,)), dma((16,)), dma,
+        ],
+        compiler_params=pltpu.CompilerParams(collective_id=2, has_side_effects=True, vmem_limit_bytes=VMEM_CAP),
+        name="backward_step",
+    )(*big, *experts, *little, prefix)
 
 
 def shards(
@@ -314,7 +1410,92 @@
     )
 
 
+def fast_shards(
+    inputs,
+    attn_gain,
+    w_query,
+    w_key,
+    w_value,
+    w_output,
+    centroids,
+    norm1_gain,
+    norm2_gain,
+    up_first,
+    down_first,
+    up_second,
+    down_second,
+    routes,
+    prefix,
+    cotangent,
+):
+    zs = lax.axis_size("grp") // 4
+    group_total = lax.axis_size("grp")
+    ep_size = lax.axis_size("ep")
+    per = w_query.shape[0]
+    tokens, width = inputs.shape
+    extra = jnp.concatenate([attn_gain[None, :], centroids.T], axis=0)
+    extra = jnp.pad(extra, ((0, 16 - extra.shape[0]), (0, 128 - per)))
+    full = gather_weights(zs, [w_query, w_key, w_value, w_output, extra])
+    mats = [f.reshape(width, width) for f in full[:4]]
+    extras = full[4].reshape(width // per, 16, 128)[:, :3, :per].transpose(1, 0, 2).reshape(3, width)
+    gain, cents = extras[0:1], extras[1:3]
+    attn_in, queries, keys, values, context, hidden, gate, pick, slot_rows, slot_grads, branch_sq = attend(
+        HEADS, inputs, gain, *mats, cents, routes, prefix, cotangent
+    )
+
+    def swap(rows):
+        return lax.all_to_all(
+            rows.reshape(ep_size, tokens, width), "ep", split_axis=0, concat_axis=0, tiled=True
+        ).reshape(ep_size * tokens, width)
+
+    rows = swap(slot_rows)
+    grads = swap(slot_grads)
+    gain1, gain2 = norm1_gain, norm2_gain
+    weights = (up_first, down_first, up_second, down_second)
+    in_one, in_two, act_one, slope_one, act_two, slope_two, middle, delta, sub_sq = expert_forward(
+        rows, gain1, gain2, *weights
+    )
+    pieces = lambda a: a.reshape(ep_size, tokens, width)
+    reduced = backward_step(
+        zs,
+        HEADS,
+        [inputs, attn_in, queries, keys, values, context, cotangent, hidden, pick, *mats],
+        [act_one, act_two, slope_one, slope_two, pieces(in_one), pieces(in_two), pieces(grads), pieces(rows),
+         pieces(delta), middle, *weights],
+        [gain, cents, gain1, gain2, gate, routes, branch_sq, sub_sq],
+        prefix.reshape(1, 1),
+    )
+    result, input_grad = reduced[7:9]
+    down_two_sum, up_two_sum, down_one_sum, up_one_sum = (reduced[0][i] for i in range(4))
+    query_sum, key_sum, value_sum, output_sum = reduced[1:5]
+    grp_sum, all_sum = reduced[5], reduced[6]
+    grp_at = lax.axis_index("grp") * (width // group_total)
+    all_at = (lax.axis_index("grp") * ep_size + lax.axis_index("ep")) * per
+    gains = lax.dynamic_slice(grp_sum, (0, grp_at), (2, width // group_total))
+    outer = lax.dynamic_slice(all_sum, (0, all_at), (5, per))
+    cell_count = float(tokens * width * group_total * ep_size)
+    rms_values = jnp.sqrt(jnp.sum(all_sum[5:9], axis=1) / cell_count)
+    return (
+        result,
+        input_grad,
+        outer[2],
+        query_sum,
+        key_sum,
+        value_sum,
+        output_sum,
+        outer[3:5].T,
+        gains[0:1],
+        gains[1:2],
+        up_one_sum.T[None],
+        down_one_sum[None],
+        up_two_sum.T[None],
+        down_two_sum[None],
+        rms_values,
+    )
+
+
 def solution(mesh):
+    fast = mesh.shape["ep"] == 2 and mesh.shape["grp"] == 16
     in_specs = (
         P(("grp", "ep"), None),
         P(("grp", "ep")),
@@ -350,4 +1531,4 @@
         P("ep", "grp", None),
         P(),
     )
-    return jax.shard_map(shards, mesh=mesh, in_specs=in_specs, out_specs=out_specs, check_vma=False)
+    return jax.shard_map(fast_shards if fast else shards, mesh=mesh, in_specs=in_specs, out_specs=out_specs, check_vma=False)

time: 1760 us -> 471 us (0.27)
  waiting for transfers between devices: 1300 us -> 0.01 us
  Pallas kernels: 0 us -> 423 us
  matrix products: 193 us -> 0 us
  blocking collectives: 184 us -> 18.2 us
  other arithmetic: 24.1 us -> 2.76 us
    reduce_scatter x12 -> x0, waiting for transfers between devices: 1010 us -> none  [the longest x1 183 us: shards(): lax.psum_scatter(grad_up_one[None], 'grp', scatter_dimension=2, tiled=True)]
    pallas_call x0 -> x4, Pallas kernels: none -> 423 us  [the longest x1 308 us: backward_step(): pl.pallas_call(functools.partial(step_kernel, zs, heads), out_shape=outs,...]
    dot_general x32 -> x0, matrix products: 190 us -> none  [the longest x9 71.4 us: matmul(): return jnp.dot(left_side, right_side, preferred_element_type=jnp.float32)]
    all_gather x4 -> x0, waiting for transfers between devices: 175 us -> none  [the longest x1 55.8 us: shards(): lax.all_gather(w_query, ('grp', 'ep'), axis=0, tiled=True)]
    unnamed x24 -> x0, waiting for transfers between devices: 80.4 us -> none
    unnamed x3 -> x0, blocking collectives: 74.4 us -> none
    all_gather x1 -> x0, blocking collectives: 68 us -> none  [shards(): lax.all_gather(centroids, ('grp', 'ep'), axis=0, tiled=True)]
    psum x1 -> x0, blocking collectives: 42 us -> none  [shards(): square_totals = lax.psum(square_terms, ('grp', 'ep'))]
  transfers between devices with their start and end apart: 24 -> 1, of which waited for: 18 -> 0; matrix products, arithmetic and copies ran while one was open for 7% -> 0% of each run, Pallas kernels for 0% -> 8%
where the time goes in v1:
time: 471 us; the launch traced here: 469 us
  Pallas kernels  423 us (90%)
  local copies, waits for them, and re-layouts  18.8 us (4%)
  blocking collectives  18.2 us (4%)
    pallas_call x1, Pallas kernels, backward_step(): pl.pallas_call(functools.partial(step_kernel, zs, heads), out_shape=outs,...  308 us
    pallas_call x1, Pallas kernels, gather_weights(): pl.pallas_call(functools.partial(gather_kernel, zs), out_shape=shapes, in...  60.7 us
    pallas_call x1, Pallas kernels, expert_forward(): pl.pallas_call(functools.partial(expert_forward_kernel, tiles), grid=(2,...  38.3 us
    all_to_all x1, blocking collectives, swap(): lax.all_to_all(rows.reshape(ep_size, tokens, width), 'ep', split_axis=0,...  18.2 us
    pallas_call x1, Pallas kernels, attend(): pl.pallas_call(functools.partial(attend_kernel, heads), in_specs=[vm] * 8...  16.4 us
    unnamed x20, local copies, waits for them, and re-layouts  9.57 us
  transfers between devices with their start and end apart: 1, of which 0 were waited for; matrix products, arithmetic and copies ran while one was open for 0% of the time, Pallas kernels for 8%

profile of v1, /device:TPU:1, one launch (start us, length us, event | category | flops | bytes accessed | tf_op | source)
XLA Modules:
  0.0 469.0 jit_solution(6733724225774303057)
XLA Ops:
  0.6 1.3 fusion.5.refs_4_
  1.9 60.7 %gather_weights.1 = (bf16[4,2,2,2,32,1024]{5,4,3,2,1,0:T(8,128)(2,1)}, bf16[4,2,2,2,32,1024]{5,4,3,2,1,0:T(8,128)(2,1)}, bf16[4,2,2,2,32,1024]{5,4,3,2,1,0:T(8,1...) custom-call(bf16[32,1024]{1,0:T(8,128)(2,1)} %refs_0_.2, bf16[32,1024]{1,0:T(8,128)(2,1)} %refs_1_.1, ...), custom_call_target="tpu_custom_call" | custom-call | tf_op jit(solution)/shard_map/gather_weights/pallas_call | solution.py:227
  62.6 0.9 slice.56
  63.5 0.7 slice.46.cents.refs_28_
  64.2 0.7 slice.44.gain.refs_27_
  64.9 1.5 copy.32.routes.refs_32_
  67.0 16.4 %attend.1 = (bf16[256,1024]{1,0:T(8,128)(2,1)}, bf16[256,1024]{1,0:T(8,128)(2,1)}, bf16[256,1024]{1,0:T(8,128)(2,1)}, bf16[256,1024]{1,0:T(8,128)(2,1)}, bf16[25...) custom-call(bf16[256,1024]{1,0:T(8,128)(2,1)} %refs_0_.3, ...), custom_call_target="tpu_custom_call" | custom-call | tf_op jit(solution)/shard_map/attend/pallas_call | solution.py:402
  83.4 18.2 %all_to_all.10.refs_20_ = bf16[2,256,1024]{2,1,0:T(8,128)(2,1)} all-to-all(bf16[2,256,1024]{2,1,0:T(8,128)(2,1)} %bitcast.47), channel_id=1, replica_groups=mesh['grp'=16,'ep'=2] {'ep'}, dimensions={0} | all-to-all | bytes 2097152 | tf_op jit(solution)/shard_map/all_to_all | solution.py:1447
  101.6 4.6 all-to-all-start.1
  106.2 38.3 %expert_forward.1 = (bf16[512,1024]{1,0:T(8,128)(2,1)}, bf16[512,1024]{1,0:T(8,128)(2,1)}, bf16[512,4096]{1,0:T(8,128)(2,1)}, bf16[512,4096]{1,0:T(8,128)(2,1)},...) custom-call(bf16[512,1024]{1,0:T(8,128)(2,1)} %bitcast.34, ...), custom_call_target="tpu_custom_call" | custom-call | tf_op jit(solution)/shard_map/expert_forward/pallas_call | solution.py:329
  144.5 0.0 all-to-all-done.1.refs_19_
  144.5 307.8 %backward_step.1 = (f32[4,256,1024]{2,1,0:T(8,128)}, f32[32,1024]{1,0:T(8,128)}, f32[32,1024]{1,0:T(8,128)}, f32[32,1024]{1,0:T(8,128)}, f32[32,1024]{1,0:T(8,12...) custom-call(bf16[256,1024]{1,0:T(8,128)(2,1)} %refs_0_.3, ...), custom_call_target="tpu_custom_call" | custom-call | tf_op jit(solution)/shard_map/backward_step/pallas_call | solution.py:1118
  452.3 0.8 constant_dynamic-slice_fusion.1
  453.1 0.6 slice_bitcast_fusion.2
  453.7 0.5 slice_bitcast_fusion.3
  454.2 1.0 slice_reduce_fusion
  455.1 3.9 fusion.6
  459.1 0.0 copy-start
  459.1 0.0 copy-start.3
  459.1 0.0 copy-start.2
  459.1 0.0 copy-start.1
  459.1 1.3 copy.34
  460.4 0.0 copy-start.4
  460.4 1.3 copy.35
  461.7 0.7 constant_dynamic-slice_fusion
  462.5 0.5 fusion.7
  463.0 0.5 multiply_sqrt_fusion
  463.5 1.9 copy.46
  465.4 0.0 copy-done
  465.4 1.0 copy.47
  466.3 0.0 copy-done.4
  466.4 0.7 copy.48
  467.0 0.0 copy-done.3
  467.0 0.7 copy.49
  467.7 0.0 copy-done.2
  467.7 0.7 copy.50
  468.3 0.0 copy-done.1
  468.3 0.7 copy.51
  (3 shorter events, 0.0 us)
Async XLA Ops:
  101.6 42.9 %all-to-all-start.1 = ((bf16[2,256,1024]{2,1,0:T(8,128)(2,1)}), bf16[2,256,1024]{2,1,0:T(8,128)(2,1)}, u32[]{:S(2)}, u32[]{:S(2)}) async-start(bf16[2,256,1024]{2,1,0:T(8,128)(2,1)} %bitcast.46), calls=%async_computation.1 | async-start | bytes 2097152 | tf_op jit(solution)/shard_map/all_to_all | solution.py:1447
  459.1 6.3 %copy-start = (f32[256,1024]{1,0:T(8,128)S(1)}, f32[256,1024]{1,0:T(8,128)}, u32[]{:S(2)}) copy-start(f32[256,1024]{1,0:T(8,128)} %get-tuple-element.120) | copy-start | bytes 3145732
  459.1 7.9 %copy-start.3 = (f32[32,1024]{1,0:T(8,128)S(1)}, f32[32,1024]{1,0:T(8,128)}, u32[]{:S(2)}) copy-start(f32[32,1024]{1,0:T(8,128)} %get-tuple-element.123) | copy-start | bytes 393220
  459.1 8.6 %copy-start.2 = (f32[32,1024]{1,0:T(8,128)S(1)}, f32[32,1024]{1,0:T(8,128)}, u32[]{:S(2)}) copy-start(f32[32,1024]{1,0:T(8,128)} %get-tuple-element.124) | copy-start | bytes 393220
  459.1 9.2 %copy-start.1 = (f32[32,1024]{1,0:T(8,128)S(1)}, f32[32,1024]{1,0:T(8,128)}, u32[]{:S(2)}) copy-start(f32[32,1024]{1,0:T(8,128)} %get-tuple-element.125) | copy-start | bytes 393220
  460.4 5.9 %copy-start.4 = (f32[32,1024]{1,0:T(8,128)S(1)}, f32[32,1024]{1,0:T(8,128)}, u32[]{:S(2)}) copy-start(f32[32,1024]{1,0:T(8,128)} %get-tuple-element.122) | copy-start | bytes 393220

commit v2 on v1

--- a/solution.py
+++ b/solution.py
@@ -250,92 +250,139 @@
     return v * phi, phi + v * (tail * INV_ROOT_TWO_PI)
 
 
-def expert_forward_kernel(tiles, rows, gain1, gain2, up1, down1, up2, down2, in1, in2, act1, slope1, act2, slope2, middle, delta, sums, acc, sub):
+def expert_forward_kernel(tiles, slots, slot_grads, gain1, gain2, up1, down1, up2, down2, in1, in2, act1, slope1, act2, slope2, middle, delta, sums, rows, grads, acc, sub, near, stage, send_sem, recv_sem, copy_sem):
     layer = pl.program_id(0)
     t = pl.program_id(1)
+    bf, f32 = jnp.bfloat16, jnp.float32
+    z, x, core, ep = place(0)
+    y_peer = device(z, x, core, 1 - ep)
+    count = near.shape[1]
+
+    def far_rows():
+        return push(slots.at[1], rows.at[1], send_sem.at[0], recv_sem.at[0], y_peer)
+
+    def far_grads():
+        return push(slot_grads.at[1], grads.at[1], send_sem.at[1], recv_sem.at[1], y_peer)
+
+    def copy(src, dst, i):
+        return pltpu.make_async_copy(src, dst, copy_sem.at[i])
+
+    def norm_rows(half):
+        normed, _ = layer_norm(near[half].astype(f32))
+        in1[half * count : (half + 1) * count] = (normed * gain1[...].astype(f32)).astype(bf)
 
     @pl.when((layer == 0) & (t == 0))
     def _():
-        normed, _ = layer_norm(rows[...].astype(jnp.float32))
-        in1[...] = (normed * gain1[...].astype(jnp.float32)).astype(jnp.bfloat16)
-
-    def step(source, up, down, act, slope):
-        total = source.shape[0]
-        part = total
-
-        def pre_of(i):
-            return jnp.dot(source[i * part : (i + 1) * part], up[0], preferred_element_type=jnp.float32)
-
-        pre = pre_of(0)
-        for i in range(1):
-            nxt = None
-            a, s = gelu_pair(pre)
-            low = a.astype(jnp.bfloat16)
-            act[i * part : (i + 1) * part] = low
-            slope[i * part : (i + 1) * part] = s.astype(jnp.bfloat16)
-            prod = jnp.dot(low, down[0], preferred_element_type=jnp.float32)
-            span = slice(i * part, (i + 1) * part)
-
-            @pl.when(t == 0)
+        greet([y_peer])
+        far_rows().start()
+        far_grads().start()
+        copy(slots.at[0], near.at[0], 0).start()
+        copy(slot_grads.at[0], stage, 1).start()
+        copy(slots.at[0], near.at[0], 0).wait()
+        copy(slot_grads.at[0], stage, 1).wait()
+        copy(near.at[0], rows.at[0], 0).start()
+        copy(stage, grads.at[0], 1).start()
+        norm_rows(0)
+
+    @pl.when((layer == 1) & (t == 0))
+    def _():
+        copy(near.at[0], rows.at[0], 0).wait()
+        copy(stage, grads.at[0], 1).wait()
+        far_rows().wait()
+        copy(rows.at[1], near.at[1], 0).start()
+        copy(rows.at[1], near.at[1], 0).wait()
+        norm_rows(1)
+
+    def step(source, span, up, down, act, slope):
+        pre = jnp.dot(source[span], up[0], preferred_element_type=f32)
+        a, s = gelu_pair(pre)
+        low = a.astype(bf)
+        act[...] = low
+        slope[...] = s.astype(bf)
+        prod = jnp.dot(low, down[0], preferred_element_type=f32)
+
+        @pl.when(t == 0)
+        def _():
+            acc[span] = prod
+
+        @pl.when(t > 0)
+        def _():
+            acc[span] += prod
+
+    for half in range(2):
+        @pl.when(layer == half)
+        def _():
+            span = slice(half * count, (half + 1) * count)
+            step(in1, span, up1, down1, act1, slope1)
+
+            @pl.when(t == tiles - 1)
             def _():
-                acc[span] = prod
-
-            @pl.when(t > 0)
-            def _():
-                acc[span] += prod
-
-            pre = nxt
-
-    @pl.when(layer == 0)
+                value = acc[span]
+                sub[span] = value
+                square = jnp.sum(value * value, axis=0, keepdims=True)
+                if half == 0:
+                    sums[0:1] = square
+                else:
+                    sums[0:1] += square
+                mid = near[half].astype(f32) + value
+                middle[span] = mid
+                normed, _ = layer_norm(mid)
+                in2[span] = (normed * gain2[...].astype(f32)).astype(bf)
+
+    @pl.when(layer == 2)
     def _():
-        step(in1, up1, down1, act1, slope1)
-
-        @pl.when(t == tiles - 1)
-        def _():
-            value = acc[...]
-            sub[...] = value
-            sums[0:1] = jnp.sum(value * value, axis=0, keepdims=True)
-            mid = rows[...].astype(jnp.float32) + value
-            middle[...] = mid
-            normed, _ = layer_norm(mid)
-            in2[...] = (normed * gain2[...].astype(jnp.float32)).astype(jnp.bfloat16)
-
-    @pl.when(layer == 1)
-    def _():
-        step(in2, up2, down2, act2, slope2)
+        step(in2, slice(0, 2 * count), up2, down2, act2, slope2)
 
         @pl.when(t == tiles - 1)
         def _():
             value = acc[...]
             sums[1:2] = jnp.sum(value * value, axis=0, keepdims=True)
-            sums[2:8] = jnp.zeros((6, value.shape[1]), jnp.float32)
-            delta[...] = (sub[...] + value).astype(jnp.bfloat16)
-
-
-def expert_forward(rows, gain1, gain2, up1, down1, up2, down2):
-    n, feat = rows.shape
+            sums[2:8] = jnp.zeros((6, value.shape[1]), f32)
+            delta[...] = (sub[...] + value).astype(bf)
+            far_grads().wait()
+
+
+def expert_forward(slots, slot_grads, gain1, gain2, up1, down1, up2, down2):
+    _, count, feat = slots.shape
+    n = 2 * count
     hidden = up1.shape[2]
     tile = 1024
     tiles = hidden // tile
     last = tiles - 1
     bf, f32 = jnp.bfloat16, jnp.float32
     shape = jax.ShapeDtypeStruct
+    hbm = pl.BlockSpec(memory_space=pl.ANY)
     whole = lambda s: pl.BlockSpec(s, lambda l, t: (0,) * len(s))
-    first = lambda l, t: jnp.where(l == 0, t, last)
-    second = lambda l, t: jnp.where(l == 0, 0, t)
+    first = lambda l, t: jnp.where(l < 2, t, last)
+    second = lambda l, t: jnp.where(l < 2, 0, t)
     up = lambda f: pl.BlockSpec((1, feat, tile), lambda l, t: (0, 0, f(l, t)))
     down = lambda f: pl.BlockSpec((1, tile, feat), lambda l, t: (0, f(l, t), 0))
-    wide = lambda f: pl.BlockSpec((n, tile), lambda l, t: (0, f(l, t)))
+    halves = pl.BlockSpec((count, tile), lambda l, t: (jnp.minimum(l, 1), first(l, t)))
+    wide = pl.BlockSpec((n, tile), lambda l, t: (0, second(l, t)))
+    dma = pltpu.SemaphoreType.DMA
     return pl.pallas_call(
         functools.partial(expert_forward_kernel, tiles),
-        grid=(2, tiles),
-        in_specs=[whole((n, feat)), whole((1, feat)), whole((1, feat)), up(first), down(first), up(second), down(second)],
-        out_specs=[whole((n, feat))] * 2 + [wide(first)] * 2 + [wide(second)] * 2 + [whole((n, feat))] * 2 + [whole((8, feat))],
-        out_shape=[shape((n, feat), bf)] * 2 + [shape((n, hidden), bf)] * 4 + [shape((n, feat), f32), shape((n, feat), bf), shape((8, feat), f32)],
-        scratch_shapes=[pltpu.VMEM((n, feat), f32), pltpu.VMEM((n, feat), f32)],
-        compiler_params=pltpu.CompilerParams(vmem_limit_bytes=VMEM_CAP, dimension_semantics=("arbitrary", "arbitrary")),
+        grid=(3, tiles),
+        in_specs=[hbm, hbm, whole((1, feat)), whole((1, feat)), up(first), down(first), up(second), down(second)],
+        out_specs=[whole((n, feat))] * 2 + [halves] * 2 + [wide] * 2 + [whole((n, feat))] * 2 + [whole((8, feat)), hbm, hbm],
+        out_shape=[shape((n, feat), bf)] * 2
+        + [shape((n, hidden), bf)] * 4
+        + [shape((n, feat), f32), shape((n, feat), bf), shape((8, feat), f32)]
+        + [shape((2, count, feat), bf)] * 2,
+        scratch_shapes=[
+            pltpu.VMEM((n, feat), f32),
+            pltpu.VMEM((n, feat), f32),
+            pltpu.VMEM((2, count, feat), bf),
+            pltpu.VMEM((count, feat), bf),
+            dma((2,)),
+            dma((2,)),
+            dma((2,)),
+        ],
+        compiler_params=pltpu.CompilerParams(
+            collective_id=3, has_side_effects=True, vmem_limit_bytes=VMEM_CAP, dimension_semantics=("arbitrary", "arbitrary")
+        ),
         name="expert_forward",
-    )(rows, gain1, gain2, up1, down1, up2, down2)
+    )(slots, slot_grads, gain1, gain2, up1, down1, up2, down2)
 
 
 def attend_kernel(heads, x, gain, wq, wk, wv, wo, cents, routes, prefix, cotangent, attn_in, queries, keys, values, context, hidden, gate, pick, slot_rows, slot_grads, sums, ctx):
@@ -384,7 +431,8 @@
     tri = (col_ids <= row_ids).astype(bf)
     count = jnp.dot(tri, hot.astype(bf), preferred_element_type=f32)
     position = jnp.sum(count * hot, axis=1, keepdims=True) - 1.0
-    target = routes[...] * tokens + position.astype(jnp.int32)
+    away = (routes[...] != lax.axis_index("ep")).astype(jnp.int32)
+    target = away * tokens + position.astype(jnp.int32)
     slots = lax.broadcasted_iota(jnp.int32, (tokens, 2 * tokens), 1)
     chosen = (slots == target).astype(bf)
     pick[...] = chosen
@@ -414,7 +462,9 @@
 
 
 SLICES = 4
+X_SLICES = 1
 LEAD = 2
+LAG = 3
 RING = 8
 
 
@@ -429,7 +479,7 @@
     (send, xrecv, zrecv, acc, tiles, sides, prod, ep_in, x_in, z_in, small_in, small_ref) = refs[54:66]
     (wd, wu, sl, ps, hb, accf, midf, loadf, picks) = refs[66:75]
     (wf_s, wf_r, nf_s, nf_r, xs, xr, zsem_s, zsem_r, es, er, axs, axr, azs, azr, ss, sr, tile_sem, side_sem) = refs[75:93]
-    (af_s, af_r, y_s, y_r, w_sem, ps_sem, ld_sem, out_sem) = refs[93:]
+    (af_s, af_r, y_s, y_r, w_sem, ps_sem, ld_sem, out_sem, free_sem) = refs[93:]
     wide = (act_two, pre_two, act_one, pre_one)
     narrow = (grads, in_two, sub_grad, in_one)
     bf, f32 = jnp.bfloat16, jnp.float32
@@ -452,18 +502,28 @@
 
     def dest(k):
         to_right = zs - 1 - z
-        d = jnp.where(k < to_right, zs - 1 - k, k - to_right)
-        return jnp.where(k < zs - 1, d, z)
+        lower = jnp.where(k < to_right, zs - 1 - k, k - to_right)
+        upper = jnp.where(k < z, k, zs - 1 - (k - z))
+        return jnp.where(k < zs - 1, jnp.where(z < zs // 2, lower, upper), z)
 
     def begins(d):
         return ((d > z) & (z == 0)) | ((d < z) & (z == zs - 1))
 
-    def fetch(pairs):
-        copies = [pltpu.make_async_copy(src, dst, ld_sem.at[i]) for i, (src, dst) in enumerate(pairs)]
+    def loads(pairs, at=0):
+        return [pltpu.make_async_copy(src, dst, ld_sem.at[at + i]) for i, (src, dst) in enumerate(pairs)]
+
+    def begin(copies):
         for c in copies:
             c.start()
+
+    def end(copies):
         for c in copies:
             c.wait()
+
+    def fetch(pairs):
+        copies = loads(pairs)
+        begin(copies)
+        end(copies)
 
     def two(slot):
         return hb.at[pl.ds(slot, 2)]
@@ -496,10 +556,10 @@
         return push(src, attn_far.at[i], af_s.at[i], af_r.at[i], c_peer)
 
     def far_delta():
-        return push(delta.at[1 - ep], back_far, y_s.at[0], y_r.at[0], y_peer)
+        return push(delta.at[1], back_far, y_s.at[0], y_r.at[0], y_peer)
 
     def far_rows():
-        return push(row_grad.at[1 - ep], grad_far, y_s.at[1], y_r.at[1], y_peer)
+        return push(row_grad, grad_far, y_s.at[1], y_r.at[1], y_peer)
 
     far_narrow(0).start()
     send_wide(0)
@@ -550,7 +610,9 @@
         return pl.ds(pl.multiple_of(s * size, size), size)
 
     def x_copy(b, s):
-        return push(send.at[lax.rem(b, RING), span(s), :], xrecv.at[b, span(s), :], xs.at[b, s], xr.at[b, s], x_peer)
+        wide_size = chunk // X_SLICES
+        at = pl.ds(pl.multiple_of(s * wide_size, wide_size), wide_size)
+        return push(send.at[lax.rem(b, RING), at, :], xrecv.at[lax.rem(b, RING), at, :], xs.at[b, s], xr.at[b, s], x_peer)
 
     def z_copy(b, s):
         w = lax.div(b, zs)
@@ -621,50 +683,78 @@
         def _():
             load_tile(lax.div(b + 1, zs), q_second(b + 1), 5 - slot)
 
-        acc[...] = product(w, slot)
+        keep = lax.rem(b, LAG + 1)
+        acc[keep] = product(w, slot)
 
         def piece(s, carry):
             sp = span(s)
-            x_copy(b, s).wait()
-            acc[sp, :] += xrecv[b, sp, :].astype(f32)
-
-            @pl.when(d != z)
+            per_x = SLICES // X_SLICES
+
+            @pl.when(lax.rem(s, per_x) == 0)
             def _():
-                @pl.when(jnp.logical_not(begins(d)))
-                def _():
-                    acc[sp, :] += z_wait(w, d, s)
-
-                send[mine, sp, :] = acc[sp, :].astype(bf)
+                x_copy(b, lax.div(s, per_x)).wait()
+
+            total = acc[keep, sp, :] + xrecv[mine, sp, :].astype(f32)
+            acc[keep, sp, :] = total
+
+            @pl.when(begins(d))
+            def _():
+                send[mine, sp, :] = total.astype(bf)
+
+            return carry
+
+        lax.fori_loop(0, SLICES, piece, 0)
+
+        @pl.when(b < blocks - RING)
+        def _():
+            pl.semaphore_signal(free_sem, inc=1, device_id=x_peer, device_id_type=MESH)
+
+        @pl.when(begins(d))
+        def _():
+            for s in range(SLICES):
+                z_copy(b, s).start()
+
+    def stage_three(b):
+        w = lax.div(b, zs)
+        d = dest(lax.rem(b, zs))
+        mine = lax.rem(b, RING)
+        keep = lax.rem(b, LAG + 1)
+
+        @pl.when((d != z) & jnp.logical_not(begins(d)))
+        def _():
+            def piece(s, carry):
+                sp = span(s)
+                send[mine, sp, :] = (acc[keep, sp, :] + z_wait(w, d, s)).astype(bf)
 
                 @pl.when(s > 0)
                 def _():
                     z_copy(b, s - 1).start()
 
-            @pl.when(d == z)
-            def _():
-                acc[sp, :] += z_wait(w, jnp.where(z > 0, z, zs), s)
+                return carry
+
+            lax.fori_loop(0, SLICES, piece, 0)
+            z_copy(b, SLICES - 1).start()
+
+        @pl.when(d == z)
+        def _():
+            def piece(s, carry):
+                sp = span(s)
+                acc[keep, sp, :] += z_wait(w, jnp.where(z > 0, z, zs), s)
 
                 @pl.when((z > 0) & (z < zs - 1))
                 def _():
-                    acc[sp, :] += z_wait(w, zs, s)
-
-            return carry
-
-        lax.fori_loop(0, SLICES, piece, 0)
-
-        @pl.when(d != z)
-        def _():
-            z_copy(b, SLICES - 1).start()
-
-        @pl.when(d == z)
-        def _():
-            copy = pltpu.make_async_copy(acc, out_w.at[w], out_sem)
+                    acc[keep, sp, :] += z_wait(w, zs, s)
+
+                return carry
+
+            lax.fori_loop(0, SLICES, piece, 0)
+            copy = pltpu.make_async_copy(acc.at[keep], out_w.at[w], out_sem)
             copy.start()
             copy.wait()
 
     tile = wd.shape[1]
 
-    def stream(source, start, count, up, down, slope, pre):
+    def stream(source, start, count, up, down, slope, pre, low_step, high_step):
         def copies(t, slot):
             cols = pl.ds(pl.multiple_of(t * tile, tile), tile)
             return (
@@ -677,8 +767,7 @@
             cols = pl.ds(pl.multiple_of(t * tile, tile), tile)
             return pltpu.make_async_copy(ps.at[slot, pl.ds(0, count), :], pre.at[pl.ds(start, count), cols], ps_sem.at[slot])
 
-        steps = hidden // tile
-        for c in copies(0, 0):
+        for c in copies(low_step, low_step % 2):
             c.start()
 
         def body(t, carry):
@@ -686,7 +775,7 @@
             for c in copies(t, slot):
                 c.wait()
 
-            @pl.when(t + 1 < steps)
+            @pl.when(t + 1 < high_step)
             def _():
                 for c in copies(t + 1, 1 - slot):
                     c.start()
@@ -694,7 +783,7 @@
             g = lax.dot_general(source(), wd[slot], last_dims, preferred_element_type=f32)
             low = (g * sl[slot, 0:count].astype(f32)).astype(bf)
 
-            @pl.when(t >= 2)
+            @pl.when(t >= low_step + 2)
             def _():
                 out(t - 2, slot).wait()
 
@@ -712,9 +801,9 @@
 
             return carry
 
-        lax.fori_loop(0, steps, body, 0)
-        out(steps - 2, lax.rem(steps - 2, 2)).wait()
-        out(steps - 1, lax.rem(steps - 1, 2)).wait()
+        lax.fori_loop(low_step, high_step, body, 0)
+        for t in range(high_step - 2, high_step):
+            out(t, t % 2).wait()
 
     part = 64
 
@@ -726,10 +815,40 @@
         mean_dot = jnp.mean(q * normed, axis=-1, keepdims=True)
         return total, inverse * (q - mean_q - normed * mean_dot)
 
-    def event_second():
-        fetch([(grads, two(0)), (middle, loadf), (rows_ref, two(2))])
-        stream(lambda: flat(0), 0, rows, up2, down2, slope_two, pre_two)
+    steps = hidden // tile
+    part_loads = loads(
+        [
+            (cot_ref, hb.at[1]),
+            (attn_in_ref, hb.at[0]),
+            (q_ref, hb.at[12]),
+            (k_ref, hb.at[13]),
+            (v_ref, hb.at[14]),
+            (x_ref, hb.at[11]),
+            (hidden_ref, loadf.at[pl.ds(0, tokens)]),
+            (pick_ref, picks),
+        ]
+    )
+    late_loads = loads(
+        [
+            (delta.at[0], hb.at[3]),
+            (context_ref, hb.at[2]),
+            (wo.at[pl.ds(0, feat // 2)], wd.at[0]),
+            (wo.at[pl.ds(feat // 2, feat // 2)], wd.at[1]),
+            (back_far, hb.at[5]),
+        ],
+        8,
+    )
+    expert_loads = loads([(middle, loadf), (rows_ref, two(2))], 14)
+
+    def event_second_start():
+        fetch([(grads, two(0))])
+        begin(expert_loads)
+        stream(lambda: flat(0), 0, rows, up2, down2, slope_two, pre_two, 0, steps // 2)
+
+    def event_second_end():
+        stream(lambda: flat(0), 0, rows, up2, down2, slope_two, pre_two, steps // 2, steps)
         send_wide(1)
+        end(expert_loads)
         small_ref[...] = jnp.zeros_like(small_ref)
         gain_row = gain2[...].astype(f32)
         per_block = tokens // part
@@ -748,10 +867,13 @@
         fetch([(two(4), sub_grad)])
         far_narrow(2).start()
         send_wide(2)
-
-    def event_first(blk):
-        start = pl.multiple_of(blk * tokens, tokens)
-        stream(lambda: hb[4 + blk], start, tokens, up1, down1, slope_one, pre_one)
+        begin(part_loads)
+
+    def first_stream(blk, low_step, high_step):
+        start = blk * tokens
+        stream(lambda: hb[4 + blk], start, tokens, up1, down1, slope_one, pre_one, low_step, high_step)
+
+    def first_norm(blk):
         gain_row = gain1[...].astype(f32)
 
         def body(i, carry):
@@ -764,46 +886,45 @@
             return carry
 
         lax.fori_loop(0, tokens // part, body, 0)
-        fetch([(hb.at[6 + blk], row_grad.at[blk])])
-
-    def event_first_far():
-        event_first(1 - ep)
+
+    def event_far_start():
+        first_stream(1, 0, steps // 2)
+
+    def event_far_end():
+        first_stream(1, steps // 2, steps)
+        first_norm(1)
+        fetch_out = pltpu.make_async_copy(hb.at[7], row_grad, out_sem)
+        fetch_out.start()
+        fetch_out.wait()
         far_rows().start()
 
-    def event_first_own():
-        event_first(ep)
+    def event_own_start():
+        first_stream(0, 0, steps // 2)
+
+    def event_own_end():
+        first_stream(0, steps // 2, steps)
+        first_norm(0)
         send_wide(3)
-
-    def event_attend():
         far_delta().wait_recv()
+        begin(late_loads)
+
+    half = feat // 2
+
+    def event_combine():
         far_rows().wait_recv()
-        fetch(
-            [
-                (cot_ref, hb.at[1]),
-                (delta.at[ep], hb.at[3]),
-                (back_far, hb.at[5]),
-                (row_grad.at[ep], hb.at[7]),
-                (grad_far, hb.at[9]),
-                (q_ref, hb.at[12]),
-                (k_ref, hb.at[13]),
-                (v_ref, hb.at[14]),
-                (x_ref, hb.at[11]),
-                (attn_in_ref, hb.at[0]),
-                (context_ref, hb.at[2]),
-                (hidden_ref, loadf.at[pl.ds(0, tokens)]),
-                (pick_ref, picks),
-                (wo.at[pl.ds(0, feat // 2)], wd.at[0]),
-                (wo.at[pl.ds(feat // 2, feat // 2)], wd.at[1]),
-            ]
-        )
+        row_load = pltpu.make_async_copy(grad_far, hb.at[9], out_sem)
+        row_load.start()
+        end(part_loads)
+        end(late_loads)
+        row_load.wait()
         c = cents[...].astype(f32)
 
         def combine(i, carry):
             at = pl.ds(pl.multiple_of(i * part, part), part)
-            own = picks[at, pl.ds(pl.multiple_of(ep * tokens, tokens), tokens)]
-            far = picks[at, pl.ds(pl.multiple_of((1 - ep) * tokens, tokens), tokens)]
+            own = picks[at, 0:tokens]
+            far = picks[at, tokens : 2 * tokens]
             returned = jnp.dot(own, hb[3], preferred_element_type=f32) + jnp.dot(far, hb[5], preferred_element_type=f32)
-            back = jnp.dot(own, hb[7], preferred_element_type=f32) + jnp.dot(far, hb[9], preferred_element_type=f32)
+            back = jnp.dot(own, hb[6], preferred_element_type=f32) + jnp.dot(far, hb[9], preferred_element_type=f32)
             g = gate[at]
             hid = loadf[at]
             res = hid + g * returned
@@ -823,11 +944,12 @@
 
         lax.fori_loop(0, tokens // part, combine, 0)
         fetch([(hb.at[15], result)])
-        half = feat // 2
         for i in range(2):
             hb[15, :, i * half : (i + 1) * half] = lax.dot_general(
                 hb[10], wd[i], last_dims, preferred_element_type=f32
             ).astype(bf)
+
+    def event_heads(low_pair, high_pair):
         row_ids = lax.broadcasted_iota(jnp.int32, (tokens, tokens), 0)
         col_ids = lax.broadcasted_iota(jnp.int32, (tokens, tokens), 1)
         pair = 2 * feat // heads
@@ -861,11 +983,13 @@
             hb[8, :, cols] = jnp.where(low_half, outs[0][2], outs[1][2]).astype(bf)
             return carry
 
-        lax.fori_loop(0, heads // 2, head, 0)
-        loads = [(m, i) for i in range(2) for m in (wq, wk, wv)]
+        lax.fori_loop(low_pair, high_pair, head, 0)
+
+    def event_inputs():
+        order = [(m, i) for i in range(2) for m in (wq, wk, wv)]
 
         def weight_copy(n):
-            m, i = loads[n]
+            m, i = order[n]
             return pltpu.make_async_copy(m.at[pl.ds(i * half, half)], wd.at[n % 2], w_sem.at[n % 2, 0])
 
         weight_copy(0).start()
@@ -894,6 +1018,8 @@
         small_ref[6:7] = branch_sq[0:1]
         small_ref[7:9] = sub_sq[0:2]
         start0()
+
+    def event_products():
         for i in range(6):
             far_attn(i, hb.at[0]).wait_recv()
         fetch(
@@ -1042,35 +1168,60 @@
             last_z(w)
         small_all[...] = end3()
 
-    events = EVENTS(
-        event_second, event_first_far, event_first_own, event_attend, event_x, event_small1, event_small2, event_small3,
-        event_z, event_last,
-    )
+    pairs = heads // 2
+    steps_at = [
+        (1, event_second_start),
+        (2, event_second_end),
+        (3, event_far_start),
+        (4, event_far_end),
+        (5, event_own_start),
+        (6, event_own_end),
+        (7, event_combine),
+        (8, lambda: event_heads(0, pairs // 2)),
+        (9, lambda: event_heads(pairs // 2, pairs)),
+        (10, event_inputs),
+        (11, event_products),
+        (11, event_small1),
+        (12, event_small2),
+        (13, event_small3),
+    ]
+    steps_at += [(12 + w, event_x(w)) for w in range(4)]
+    steps_at += [(14 + w, event_z(w)) for w in range(4)]
 
     def pipeline(t, carry):
-        for at, action in events:
+        @pl.when(t < blocks)
+        def _():
+            stage_one(t)
+
+        @pl.when((t > 0) & (t <= blocks))
+        def _():
+            @pl.when(t - 1 >= RING)
+            def _():
+                pl.semaphore_wait(free_sem, 1)
+
+            for s in range(X_SLICES):
+                x_copy(t - 1, s).start()
+
+        for at, action in steps_at:
             pl.when(t == at)(action)
 
-        @pl.when(t < blocks)
-        def _():
-            stage_one(t)
-
-        @pl.when((t > 0) & (t <= blocks))
-        def _():
-            for s in range(SLICES):
-                x_copy(t - 1, s).start()
-
         @pl.when(t == LEAD - 1)
         def _():
             load_tile(0, q_second(0), 2)
 
-        @pl.when(t >= LEAD)
+        @pl.when((t >= LEAD) & (t < blocks + LEAD))
         def _():
             stage_two(t - LEAD)
 
+        late = t - LEAD - jnp.where((z == 0) | (z == zs - 1), LAG, LAG - 1)
+
+        @pl.when((late >= 0) & (late < blocks))
+        def _():
+            stage_three(late)
+
         return carry
 
-    lax.fori_loop(0, blocks + LEAD, pipeline, 0)
+    lax.fori_loop(0, blocks + LEAD + LAG, pipeline, 0)
     event_last()
 
     def drain(b, carry):
@@ -1083,14 +1234,6 @@
         all_far(w).wait_send()
     far_delta().wait_send()
     far_rows().wait_send()
-
-
-def EVENTS(second, first_far, first_own, attend_event, x_of, small1, small2, small3, z_of, last):
-    found = [(2, second), (5, first_far), (7, first_own), (9, attend_event)]
-    found += [(11, small1), (12, small2), (13, small3)]
-    found += [(11 + w, x_of(w)) for w in range(4)]
-    found += [(14 + w, z_of(w)) for w in range(4)]
-    return found
 
 
 def backward_step(zs, heads, big, experts, little, prefix):
@@ -1108,7 +1251,7 @@
     outs += [shape((per, feat), f32)] * 4
     outs += [shape((16, feat), f32)] * 2
     outs += [shape((tokens, feat), bf), shape((tokens, feat), f32)]
-    outs += [shape((rows, hidden), bf)] * 2 + [shape((2, tokens, feat), bf)] * 2
+    outs += [shape((rows, hidden), bf)] * 2 + [shape((2, tokens, feat), bf), shape((tokens, feat), bf)]
     outs += [shape((4, 2 * zs, rows, chunk), bf), shape((4, 2, tokens, feat), bf), shape((6, tokens, feat), bf)]
     outs += [shape((tokens, feat), bf)] * 2
     s = SLICES
@@ -1122,9 +1265,9 @@
         out_specs=[hbm] + [vm] * 6 + [hbm] * 11,
         scratch_shapes=[
             vmem((RING, chunk, feat), bf),
-            vmem((blocks, chunk, feat), bf),
+            vmem((RING, chunk, feat), bf),
             vmem((4, zs + 1, chunk, feat), bf),
-            vmem((chunk, feat), f32),
+            vmem((LAG + 1, chunk, feat), f32),
             vmem((4, 2 * rows, chunk), bf),
             vmem((2, 4, tokens, feat), bf),
             vmem((4, zs, 2, 2, per, feat), bf),
@@ -1146,7 +1289,7 @@
             dma((blocks, s)), dma((blocks, s)), dma((blocks, s)), dma((4, zs + 1, s)),
             dma((4,)), dma((4,)), dma((4,)), dma((4,)), dma((4, zs)), dma((4, zs + 1)),
             dma((4, zs)), dma((4, zs)), dma((4, 2)), dma((2,)),
-            dma((6,)), dma((6,)), dma((2,)), dma((2,)), dma((2, 3)), dma((2,)), dma((16,)), dma,
+            dma((6,)), dma((6,)), dma((2,)), dma((2,)), dma((2, 3)), dma((2,)), dma((16,)), dma, pltpu.SemaphoreType.REGULAR,
         ],
         compiler_params=pltpu.CompilerParams(collective_id=2, has_side_effects=True, vmem_limit_bytes=VMEM_CAP),
         name="backward_step",
@@ -1443,24 +1586,17 @@
         HEADS, inputs, gain, *mats, cents, routes, prefix, cotangent
     )
 
-    def swap(rows):
-        return lax.all_to_all(
-            rows.reshape(ep_size, tokens, width), "ep", split_axis=0, concat_axis=0, tiled=True
-        ).reshape(ep_size * tokens, width)
-
-    rows = swap(slot_rows)
-    grads = swap(slot_grads)
     gain1, gain2 = norm1_gain, norm2_gain
     weights = (up_first, down_first, up_second, down_second)
-    in_one, in_two, act_one, slope_one, act_two, slope_two, middle, delta, sub_sq = expert_forward(
-        rows, gain1, gain2, *weights
+    in_one, in_two, act_one, slope_one, act_two, slope_two, middle, delta, sub_sq, rows, grads = expert_forward(
+        slot_rows.reshape(2, tokens, width), slot_grads.reshape(2, tokens, width), gain1, gain2, *weights
     )
     pieces = lambda a: a.reshape(ep_size, tokens, width)
     reduced = backward_step(
         zs,
         HEADS,
         [inputs, attn_in, queries, keys, values, context, cotangent, hidden, pick, *mats],
-        [act_one, act_two, slope_one, slope_two, pieces(in_one), pieces(in_two), pieces(grads), pieces(rows),
+        [act_one, act_two, slope_one, slope_two, pieces(in_one), pieces(in_two), grads, rows,
          pieces(delta), middle, *weights],
         [gain, cents, gain1, gain2, gate, routes, branch_sq, sub_sq],
         prefix.reshape(1, 1),

time: 471 us -> 395 us (0.84)
  Pallas kernels: 423 us -> 371 us
  blocking collectives: 18.2 us -> 0 us
    pallas_call x1, Pallas kernels: 308 us -> 246 us  [backward_step(): pl.pallas_call(functools.partial(step_kernel, zs, heads), out_shape=outs,...]
    all_to_all x1 -> x0, blocking collectives: 18.2 us -> none  [swap(): lax.all_to_all(rows.reshape(ep_size, tokens, width), 'ep', split_axis=0,...]
    pallas_call x1, Pallas kernels: 38.3 us -> 47.2 us  [expert_forward(): pl.pallas_call(functools.partial(expert_forward_kernel, tiles), grid=(3,...]
  transfers between devices with their start and end apart: 1 -> 0, of which waited for: 0 -> 0; matrix products, arithmetic and copies ran while one was open for 0% -> 0% of each run, Pallas kernels for 8% -> 0%
where the time goes in v2:
time: 395 us; the launch traced here: 394 us
  Pallas kernels  371 us (94%)
  local copies, waits for them, and re-layouts  18.8 us (5%)
    pallas_call x1, Pallas kernels, backward_step(): pl.pallas_call(functools.partial(step_kernel, zs, heads), out_shape=outs,...  246 us
    pallas_call x1, Pallas kernels, gather_weights(): pl.pallas_call(functools.partial(gather_kernel, zs), out_shape=shapes, in...  60.7 us
    pallas_call x1, Pallas kernels, expert_forward(): pl.pallas_call(functools.partial(expert_forward_kernel, tiles), grid=(3,...  47.2 us
    pallas_call x1, Pallas kernels, attend(): pl.pallas_call(functools.partial(attend_kernel, heads), in_specs=[vm] * 8...  16.6 us
    unnamed x20, local copies, waits for them, and re-layouts  9.57 us

profile of v2, /device:TPU:1, one launch (start us, length us, event | category | flops | bytes accessed | tf_op | source)
XLA Modules:
  0.0 393.6 jit_solution(17518266711302725758)
XLA Ops:
  0.6 1.3 fusion.5.refs_4_
  1.9 60.7 %gather_weights.1 = (bf16[4,2,2,2,32,1024]{5,4,3,2,1,0:T(8,128)(2,1)}, bf16[4,2,2,2,32,1024]{5,4,3,2,1,0:T(8,128)(2,1)}, bf16[4,2,2,2,32,1024]{5,4,3,2,1,0:T(8,1...) custom-call(bf16[32,1024]{1,0:T(8,128)(2,1)} %refs_0_.2, bf16[32,1024]{1,0:T(8,128)(2,1)} %refs_1_.1, ...), custom_call_target="tpu_custom_call" | custom-call | tf_op jit(solution)/shard_map/gather_weights/pallas_call | solution.py:227
  62.6 0.9 slice.56
  63.5 0.7 slice.46.cents.refs_28_
  64.2 0.7 slice.44.gain.refs_27_
  64.9 1.5 copy.32.routes.refs_32_
  67.0 16.6 %attend.1 = (bf16[256,1024]{1,0:T(8,128)(2,1)}, bf16[256,1024]{1,0:T(8,128)(2,1)}, bf16[256,1024]{1,0:T(8,128)(2,1)}, bf16[256,1024]{1,0:T(8,128)(2,1)}, bf16[25...) custom-call(bf16[256,1024]{1,0:T(8,128)(2,1)} %refs_0_.3, ...), custom_call_target="tpu_custom_call" | custom-call | tf_op jit(solution)/shard_map/attend/pallas_call | solution.py:450
  83.6 47.2 %expert_forward.1 = (bf16[512,1024]{1,0:T(8,128)(2,1)}, bf16[512,1024]{1,0:T(8,128)(2,1)}, bf16[512,4096]{1,0:T(8,128)(2,1)}, bf16[512,4096]{1,0:T(8,128)(2,1)},...) custom-call(bf16[2,256,1024]{2,1,0:T(8,128)(2,1)} %bitcast.44, ...), custom_call_target="tpu_custom_call" | custom-call | tf_op jit(solution)/shard_map/expert_forward/pallas_call | solution.py:363
  130.8 246.2 %backward_step.1 = (f32[4,256,1024]{2,1,0:T(8,128)}, f32[32,1024]{1,0:T(8,128)}, f32[32,1024]{1,0:T(8,128)}, f32[32,1024]{1,0:T(8,128)}, f32[32,1024]{1,0:T(8,12...) custom-call(bf16[256,1024]{1,0:T(8,128)(2,1)} %refs_0_.3, ...), custom_call_target="tpu_custom_call" | custom-call | tf_op jit(solution)/shard_map/backward_step/pallas_call | solution.py:1261
  377.0 3.9 %fusion.6 = (f32[1,256,1024]{2,1,0:T(8,128)}, f32[1,1024,256]{1,2,0:T(8,128)S(1)}, f32[1,256,1024]{2,1,0:T(8,128)}, f32[1,1024,256]{1,2,0:T(8,128)S(1)}) fusion(f32[4,256,1024]{2,1,0:T(8,128)} %get-tuple-element.86), kind=kLoop, calls=%fused_computation.17 | loop fusion | bytes 8388608 | tf_op jit(solution)/shard_map/slice | solution.py:1605
  380.9 0.0 copy-start
  380.9 0.0 copy-start.3
  380.9 0.0 copy-start.2
  380.9 0.0 copy-start.1
  380.9 1.3 copy.34
  382.2 0.0 copy-start.4
  382.2 1.3 copy.35
  383.5 0.8 constant_dynamic-slice_fusion.1
  384.3 0.6 slice_bitcast_fusion.2
  384.9 0.5 slice_bitcast_fusion.3
  385.4 0.8 constant_dynamic-slice_fusion
  386.1 0.5 fusion.7
  386.7 1.0 slice_reduce_fusion
  387.6 0.5 multiply_sqrt_fusion
  388.1 1.9 copy.46
  390.0 0.0 copy-done
  390.0 1.0 copy.47
  391.0 0.0 copy-done.4
  391.0 0.7 copy.48
  391.6 0.0 copy-done.3
  391.6 0.7 copy.49
  392.3 0.0 copy-done.2
  392.3 0.7 copy.50
  393.0 0.0 copy-done.1
  393.0 0.7 copy.51
  (3 shorter events, 0.0 us)
Async XLA Ops:
  380.9 9.1 %copy-start = (f32[256,1024]{1,0:T(8,128)S(1)}, f32[256,1024]{1,0:T(8,128)}, u32[]{:S(2)}) copy-start(f32[256,1024]{1,0:T(8,128)} %get-tuple-element.124) | copy-start | bytes 3145732
  380.9 10.7 %copy-start.3 = (f32[32,1024]{1,0:T(8,128)S(1)}, f32[32,1024]{1,0:T(8,128)}, u32[]{:S(2)}) copy-start(f32[32,1024]{1,0:T(8,128)} %get-tuple-element.127) | copy-start | bytes 393220
  380.9 11.4 %copy-start.2 = (f32[32,1024]{1,0:T(8,128)S(1)}, f32[32,1024]{1,0:T(8,128)}, u32[]{:S(2)}) copy-start(f32[32,1024]{1,0:T(8,128)} %get-tuple-element.128) | copy-start | bytes 393220
  380.9 12.0 %copy-start.1 = (f32[32,1024]{1,0:T(8,128)S(1)}, f32[32,1024]{1,0:T(8,128)}, u32[]{:S(2)}) copy-start(f32[32,1024]{1,0:T(8,128)} %get-tuple-element.129) | copy-start | bytes 393220
  382.2 8.7 %copy-start.4 = (f32[32,1024]{1,0:T(8,128)S(1)}, f32[32,1024]{1,0:T(8,128)}, u32[]{:S(2)}) copy-start(f32[32,1024]{1,0:T(8,128)} %get-tuple-element.126) | copy-start | bytes 393220

commit v3 on v2

--- a/solution.py
+++ b/solution.py
@@ -96,143 +96,6 @@
     return pltpu.make_async_remote_copy(
         src_ref=src, dst_ref=dst, send_sem=send_sem, recv_sem=recv_sem, device_id=peer, device_id_type=MESH
     )
-
-
-def gather_kernel(zs, *refs):
-    shard = refs[0:5]
-    full = refs[5:10]
-    own_sem, z_send, z_recv, p_send, p_recv, c_send, c_recv = refs[10:]
-    z, x, core, ep = place(zs)
-    right = device(jnp.minimum(z + 1, zs - 1), x, core, ep)
-    left = device(jnp.maximum(z - 1, 0), x, core, ep)
-    x_peer = device(z, 1 - x, core, ep)
-    y_peer = device(z, x, core, 1 - ep)
-    c_peer = device(z, x, 1 - core, ep)
-    others = [device(lax.rem(z + k, zs), x, core, ep) for k in range(1, zs)]
-    half = shard[0].shape[1] // 2
-    items = []
-    for w in range(4):
-        items.append((w, slice(0, half), True))
-        items.append((w, slice(half, 2 * half), False))
-    items.append((4, slice(0, shard[4].shape[1]), True))
-    count = len(items)
-
-    def own(i):
-        w, cols, _ = items[i]
-        return pltpu.make_async_copy(shard[w].at[:, cols], full[w].at[z, x, core, ep, :, cols], own_sem.at[i])
-
-    def z_copy(i, src, slot, way, hop, peer):
-        w, cols, _ = items[i]
-        return push(src, full[w].at[slot, x, core, ep, :, cols], z_send.at[i, way, hop], z_recv.at[i, way, hop], peer)
-
-    def z_start(i):
-        w, cols, _ = items[i]
-
-        @pl.when(z < zs - 1)
-        def _():
-            z_copy(i, shard[w].at[:, cols], z, 0, 0, right).start()
-
-        @pl.when(z > 0)
-        def _():
-            z_copy(i, shard[w].at[:, cols], z, 1, 0, left).start()
-
-    def z_hop(i, hop):
-        w, cols, _ = items[i]
-        low = jnp.maximum(z - hop, 0)
-        high = jnp.minimum(z + hop, zs - 1)
-        from_left = full[w].at[low, x, core, ep, :, cols]
-        from_right = full[w].at[high, x, core, ep, :, cols]
-
-        @pl.when(z >= hop)
-        def _():
-            z_copy(i, from_left, low, 0, hop - 1, right).wait_recv()
-
-        if hop < zs - 1:
-            @pl.when((z >= hop) & (z < zs - 1))
-            def _():
-                z_copy(i, from_left, low, 0, hop, right).start()
-
-        @pl.when(z + hop <= zs - 1)
-        def _():
-            z_copy(i, from_right, high, 1, hop - 1, left).wait_recv()
-
-        if hop < zs - 1:
-            @pl.when((z + hop <= zs - 1) & (z > 0))
-            def _():
-                z_copy(i, from_right, high, 1, hop, left).start()
-
-    def z_drain(i):
-        w, cols, _ = items[i]
-        for hop in range(zs - 1):
-            src = full[w].at[z, x, core, ep, :, cols]
-
-            @pl.when((z < zs - 1) & (z >= hop))
-            def _():
-                z_copy(i, src, z, 0, hop, right).wait_send()
-
-            @pl.when((z > 0) & (z + hop <= zs - 1))
-            def _():
-                z_copy(i, src, z, 1, hop, left).wait_send()
-
-    def second(i):
-        w, cols, x_first = items[i]
-        part = full[w].at[:, x, core, ep, :, cols]
-        return push(part, part, p_send.at[i, 0], p_recv.at[i, 0], x_peer if x_first else y_peer)
-
-    def third(i):
-        w, cols, x_first = items[i]
-        part = full[w].at[:, :, core, ep, :, cols] if x_first else full[w].at[:, x, core, :, :, cols]
-        return push(part, part, p_send.at[i, 1], p_recv.at[i, 1], y_peer if x_first else x_peer)
-
-    def fourth(i):
-        w, cols, _ = items[i]
-        part = full[w].at[:, :, core, :, :, cols]
-        return push(part, part, c_send.at[i], c_recv.at[i], c_peer)
-
-    greet(others + [x_peer, y_peer, c_peer])
-    for i in range(count):
-        z_start(i)
-    for i in range(count):
-        own(i).start()
-    order = [[8, 0, 1], [2, 3], [4, 5], [6, 7]]
-    for t in range(len(order) + 2):
-        if t < len(order):
-            for hop in range(1, zs):
-                for i in order[t]:
-                    z_hop(i, hop)
-            for i in order[t]:
-                own(i).wait()
-                second(i).start()
-        if 1 <= t < len(order) + 1:
-            for i in order[t - 1]:
-                second(i).wait_recv()
-                third(i).start()
-        if t >= 2:
-            for i in order[t - 2]:
-                third(i).wait_recv()
-                fourth(i).start()
-    for i in range(count):
-        fourth(i).wait_recv()
-    for i in range(count):
-        z_drain(i)
-        second(i).wait_send()
-        third(i).wait_send()
-        fourth(i).wait_send()
-
-
-def gather_weights(zs, shards):
-    shapes = [jax.ShapeDtypeStruct((zs, 2, 2, 2) + s.shape, s.dtype) for s in shards]
-    n = 2 * len(shards) - 1
-    dma = pltpu.SemaphoreType.DMA
-    return pl.pallas_call(
-        functools.partial(gather_kernel, zs),
-        out_shape=shapes,
-        in_specs=[pl.BlockSpec(memory_space=pltpu.VMEM)] * len(shards),
-        out_specs=[pl.BlockSpec(memory_space=pl.ANY)] * len(shards),
-        scratch_shapes=[dma((n,)), dma((n, 2, zs)), dma((n, 2, zs)), dma((n, 2)), dma((n, 2)), dma((n,)), dma((n,))],
-        compiler_params=pltpu.CompilerParams(collective_id=1, has_side_effects=True, vmem_limit_bytes=VMEM_CAP),
-        name="gather_weights",
-    )(*shards)
 
 
 def layer_norm(v):
@@ -385,80 +248,261 @@
     )(slots, slot_grads, gain1, gain2, up1, down1, up2, down2)
 
 
-def attend_kernel(heads, x, gain, wq, wk, wv, wo, cents, routes, prefix, cotangent, attn_in, queries, keys, values, context, hidden, gate, pick, slot_rows, slot_grads, sums, ctx):
+def front_kernel(zs, heads, *refs):
+    shard = refs[0:5]
+    x, routes, cotangent, prefix = refs[5:9]
+    out_full = refs[9:13]
+    attn_in, queries, keys, values, context, hidden, gate, pick, slot_rows, slot_grads, sums, gain, cents = refs[13:26]
+    full = refs[26:31]
+    ctx, own_sem, z_send, z_recv, p_send, p_recv, c_send, c_recv, out_sem = refs[31:]
     bf, f32 = jnp.bfloat16, jnp.float32
     tokens, feat = x.shape
     pair = 2 * feat // heads
     scale = (feat // heads) ** -0.5
-    wide = x[...].astype(f32)
-    normed, _ = layer_norm(wide)
-    attn_in[...] = (normed * gain[...].astype(f32)).astype(bf)
-    for w, out in ((wq, queries), (wk, keys), (wv, values)):
-        out[...] = jnp.dot(attn_in[...], w[...], preferred_element_type=f32).astype(bf)
+    z, xx, core, ep = place(zs)
+    right = device(jnp.minimum(z + 1, zs - 1), xx, core, ep)
+    left = device(jnp.maximum(z - 1, 0), xx, core, ep)
+    x_peer = device(z, 1 - xx, core, ep)
+    y_peer = device(z, xx, core, 1 - ep)
+    c_peer = device(z, xx, 1 - core, ep)
+    others = [device(lax.rem(z + k, zs), xx, core, ep) for k in range(1, zs)]
+    half = shard[0].shape[1] // 2
+    per = shard[0].shape[0]
+    items = []
+    for w in range(4):
+        items.append((w, slice(0, half), True))
+        items.append((w, slice(half, 2 * half), False))
+    items.append((4, slice(0, shard[4].shape[1]), True))
+    count = len(items)
+
+    def own(i):
+        w, cols, _ = items[i]
+        return pltpu.make_async_copy(shard[w].at[:, cols], full[w].at[z, xx, core, ep, :, cols], own_sem.at[i])
+
+    def z_copy(i, src, slot, way, hop, peer):
+        w, cols, _ = items[i]
+        return push(src, full[w].at[slot, xx, core, ep, :, cols], z_send.at[i, way, hop], z_recv.at[i, way, hop], peer)
+
+    def z_start(i):
+        w, cols, _ = items[i]
+
+        @pl.when(z < zs - 1)
+        def _():
+            z_copy(i, shard[w].at[:, cols], z, 0, 0, right).start()
+
+        @pl.when(z > 0)
+        def _():
+            z_copy(i, shard[w].at[:, cols], z, 1, 0, left).start()
+
+    def z_hop(i, hop):
+        w, cols, _ = items[i]
+        low = jnp.maximum(z - hop, 0)
+        high = jnp.minimum(z + hop, zs - 1)
+        from_left = full[w].at[low, xx, core, ep, :, cols]
+        from_right = full[w].at[high, xx, core, ep, :, cols]
+
+        @pl.when(z >= hop)
+        def _():
+            z_copy(i, from_left, low, 0, hop - 1, right).wait_recv()
+
+        if hop < zs - 1:
+            @pl.when((z >= hop) & (z < zs - 1))
+            def _():
+                z_copy(i, from_left, low, 0, hop, right).start()
+
+        @pl.when(z + hop <= zs - 1)
+        def _():
+            z_copy(i, from_right, high, 1, hop - 1, left).wait_recv()
+
+        if hop < zs - 1:
+            @pl.when((z + hop <= zs - 1) & (z > 0))
+            def _():
+                z_copy(i, from_right, high, 1, hop, left).start()
+
+    def z_drain(i):
+        w, cols, _ = items[i]
+        for hop in range(zs - 1):
+            src = full[w].at[z, xx, core, ep, :, cols]
+
+            @pl.when((z < zs - 1) & (z >= hop))
+            def _():
+                z_copy(i, src, z, 0, hop, right).wait_send()
+
+            @pl.when((z > 0) & (z + hop <= zs - 1))
+            def _():
+                z_copy(i, src, z, 1, hop, left).wait_send()
+
+    def second(i):
+        w, cols, x_first = items[i]
+        part = full[w].at[:, xx, core, ep, :, cols]
+        return push(part, part, p_send.at[i, 0], p_recv.at[i, 0], x_peer if x_first else y_peer)
+
+    def third(i):
+        w, cols, x_first = items[i]
+        part = full[w].at[:, :, core, ep, :, cols] if x_first else full[w].at[:, xx, core, :, :, cols]
+        return push(part, part, p_send.at[i, 1], p_recv.at[i, 1], y_peer if x_first else x_peer)
+
+    def fourth(i):
+        w, cols, _ = items[i]
+        part = full[w].at[:, :, core, :, :, cols]
+        return push(part, part, c_send.at[i], c_recv.at[i], c_peer)
+
+    def put_out(w):
+        return pltpu.make_async_copy(full[w], out_full[w], out_sem.at[w])
+
+    def matrix(w):
+        return full[w][...].reshape(feat, feat)
+
+    last_dims = (((1,), (1,)), ((), ()))
+    first_dims = (((0,), (0,)), ((), ()))
+
+    def spread_extras():
+        table = full[4][...].reshape(feat // per, 16, 128)
+        lane = lax.broadcasted_iota(jnp.int32, (128, feat), 1)
+        source = lax.broadcasted_iota(jnp.int32, (128, feat), 0)
+        choose = (lax.rem(lane, per) == source).astype(bf)
+        dev = lax.broadcasted_iota(jnp.int32, (feat // per, feat), 0)
+        home = lax.div(lax.broadcasted_iota(jnp.int32, (feat // per, feat), 1), per)
+        for r in range(3):
+            spread = jnp.dot(table[:, r, :], choose, preferred_element_type=f32)
+            row = jnp.sum(jnp.where(dev == home, spread, 0.0), axis=0, keepdims=True).astype(bf)
+            if r == 0:
+                gain[...] = row
+            else:
+                cents[r - 1 : r] = row
+        normed, _ = layer_norm(x[...].astype(f32))
+        attn_in[...] = (normed * gain[...].astype(f32)).astype(bf)
+
+    def project(w):
+        out = (queries, keys, values)[w]
+        out[...] = jnp.dot(attn_in[...], matrix(w), preferred_element_type=f32).astype(bf)
+
     row_ids = lax.broadcasted_iota(jnp.int32, (tokens, tokens), 0)
     col_ids = lax.broadcasted_iota(jnp.int32, (tokens, tokens), 1)
-    visible = (col_ids <= row_ids) | (col_ids < prefix[0])
-    low_half = lax.broadcasted_iota(jnp.int32, (tokens, pair), 1) < pair // 2
-    last_dims = (((1,), (1,)), ((), ()))
-
-    def body(h, carry):
-        cols = pl.ds(pl.multiple_of(h * pair, pair), pair)
-        q, k, v = queries[:, cols], keys[:, cols], values[:, cols]
-        outs = []
-        for side in (low_half, jnp.logical_not(low_half)):
-            mine = jnp.where(side, q, jnp.zeros_like(q))
-            s = lax.dot_general(mine, k, last_dims, preferred_element_type=f32) * scale
-            s = jnp.where(visible, s, -1e30)
-            top = jnp.max(s, axis=-1, keepdims=True)
-            total = top + jnp.log(jnp.sum(jnp.exp(s - top), axis=-1, keepdims=True))
-            p = jnp.exp(s - total).astype(bf)
-            outs.append(jnp.dot(p, v, preferred_element_type=f32))
-        ctx[:, cols] = jnp.where(low_half, outs[0], outs[1]).astype(bf)
-        return carry
-
-    lax.fori_loop(0, heads // 2, body, 0)
-    context[...] = ctx[...]
-    branch = jnp.dot(ctx[...], wo[...], preferred_element_type=f32)
-    sums[...] = jnp.broadcast_to(jnp.sum(branch * branch, axis=0, keepdims=True), sums.shape)
-    hid = wide + branch
-    hidden[...] = hid
-    low = hid.astype(bf)
-    scores = lax.dot_general(low, cents[...], last_dims, preferred_element_type=f32)
-    lane = lax.broadcasted_iota(jnp.int32, scores.shape, 1)
-    hot = (lane == routes[...]).astype(f32)
-    g = 1.0 / (1.0 + jnp.exp(-jnp.sum(scores * hot, axis=1, keepdims=True)))
-    gate[...] = g
-    tri = (col_ids <= row_ids).astype(bf)
-    count = jnp.dot(tri, hot.astype(bf), preferred_element_type=f32)
-    position = jnp.sum(count * hot, axis=1, keepdims=True) - 1.0
-    away = (routes[...] != lax.axis_index("ep")).astype(jnp.int32)
-    target = away * tokens + position.astype(jnp.int32)
-    slots = lax.broadcasted_iota(jnp.int32, (tokens, 2 * tokens), 1)
-    chosen = (slots == target).astype(bf)
-    pick[...] = chosen
-    first_dims = (((0,), (0,)), ((), ()))
-    slot_rows[...] = lax.dot_general(chosen, low, first_dims, preferred_element_type=f32).astype(bf)
-    grads = (g * cotangent[...].astype(f32)).astype(bf)
-    slot_grads[...] = lax.dot_general(chosen, grads, first_dims, preferred_element_type=f32).astype(bf)
-
-
-def attend(heads, x, gain, wq, wk, wv, wo, cents, routes, prefix, cotangent):
+
+    def attention():
+        low_half = lax.broadcasted_iota(jnp.int32, (tokens, pair), 1) < pair // 2
+
+        def body(h, carry):
+            visible = (col_ids <= row_ids) | (col_ids < prefix[0])
+            cols = pl.ds(pl.multiple_of(h * pair, pair), pair)
+            q, k, v = queries[:, cols], keys[:, cols], values[:, cols]
+            outs = []
+            for side in (low_half, jnp.logical_not(low_half)):
+                mine = jnp.where(side, q, jnp.zeros_like(q))
+                s = lax.dot_general(mine, k, last_dims, preferred_element_type=f32) * scale
+                s = jnp.where(visible, s, -1e30)
+                top = jnp.max(s, axis=-1, keepdims=True)
+                total = top + jnp.log(jnp.sum(jnp.exp(s - top), axis=-1, keepdims=True))
+                p = jnp.exp(s - total).astype(bf)
+                outs.append(jnp.dot(p, v, preferred_element_type=f32))
+            ctx[:, cols] = jnp.where(low_half, outs[0], outs[1]).astype(bf)
+            return carry
+
+        lax.fori_loop(0, heads // 2, body, 0)
+        context[...] = ctx[...]
+
+    def dispatch():
+        branch = jnp.dot(ctx[...], matrix(3), preferred_element_type=f32)
+        sums[...] = jnp.broadcast_to(jnp.sum(branch * branch, axis=0, keepdims=True), sums.shape)
+        hid = x[...].astype(f32) + branch
+        hidden[...] = hid
+        low = hid.astype(bf)
+        scores = lax.dot_general(low, cents[...], last_dims, preferred_element_type=f32)
+        lane = lax.broadcasted_iota(jnp.int32, scores.shape, 1)
+        hot = (lane == routes[...]).astype(f32)
+        g = 1.0 / (1.0 + jnp.exp(-jnp.sum(scores * hot, axis=1, keepdims=True)))
+        gate[...] = g
+        tri = (col_ids <= row_ids).astype(bf)
+        counted = jnp.dot(tri, hot.astype(bf), preferred_element_type=f32)
+        position = jnp.sum(counted * hot, axis=1, keepdims=True) - 1.0
+        away = (routes[...] != ep).astype(jnp.int32)
+        target = away * tokens + position.astype(jnp.int32)
+        slots = lax.broadcasted_iota(jnp.int32, (tokens, 2 * tokens), 1)
+        chosen = (slots == target).astype(bf)
+        pick[...] = chosen
+        slot_rows[...] = lax.dot_general(chosen, low, first_dims, preferred_element_type=f32).astype(bf)
+        grads = (g * cotangent[...].astype(f32)).astype(bf)
+        slot_grads[...] = lax.dot_general(chosen, grads, first_dims, preferred_element_type=f32).astype(bf)
+
+    greet(others + [x_peer, y_peer, c_peer])
+    order = [[8, 0, 1], [2, 3], [4, 5], [6, 7]]
+    for i in order[0] + order[1]:
+        z_start(i)
+    for i in range(count):
+        own(i).start()
+    for t in range(len(order) + 3):
+        if t < len(order):
+            for hop in range(1, zs):
+                for i in order[t]:
+                    z_hop(i, hop)
+            for i in order[t]:
+                own(i).wait()
+                second(i).start()
+            if t + 2 < len(order):
+                for i in order[t + 2]:
+                    z_start(i)
+        if 1 <= t < len(order) + 1:
+            for i in order[t - 1]:
+                second(i).wait_recv()
+                third(i).start()
+
+        def pass_on():
+            for i in order[t - 2]:
+                third(i).wait_recv()
+                fourth(i).start()
+
+        if 2 <= t < len(order) + 1:
+            pass_on()
+        if t >= 3:
+            w = t - 3
+            for i in order[w]:
+                fourth(i).wait_recv()
+            put_out(w).start()
+            if w == 0:
+                spread_extras()
+            if w < 3:
+                project(w)
+            if w == 2:
+                attention()
+        if t == len(order) + 1:
+            pass_on()
+    dispatch()
+    for w in range(4):
+        put_out(w).wait()
+    for i in range(count):
+        z_drain(i)
+        second(i).wait_send()
+        third(i).wait_send()
+        fourth(i).wait_send()
+
+
+def front(zs, heads, shards_in, x, routes, cotangent, prefix):
     tokens, feat = x.shape
     bf, f32 = jnp.bfloat16, jnp.float32
     shape = jax.ShapeDtypeStruct
     vm = pl.BlockSpec(memory_space=pltpu.VMEM)
+    hbm = pl.BlockSpec(memory_space=pl.ANY)
+    n = 2 * len(shards_in) - 1
+    dma = pltpu.SemaphoreType.DMA
+    wholes = [(zs, 2, 2, 2) + s.shape for s in shards_in]
+    shapes = [shape(s, bf) for s in wholes[:4]]
+    shapes += [shape((tokens, feat), bf)] * 5
+    shapes += [shape((tokens, feat), f32), shape((tokens, 1), f32), shape((tokens, 2 * tokens), bf)]
+    shapes += [shape((2 * tokens, feat), bf)] * 2 + [shape((8, feat), f32), shape((1, feat), bf), shape((2, feat), bf)]
     return pl.pallas_call(
-        functools.partial(attend_kernel, heads),
-        in_specs=[vm] * 8 + [pl.BlockSpec(memory_space=pltpu.SMEM), vm],
-        out_specs=[vm] * 11,
-        out_shape=[shape((tokens, feat), bf)] * 5
-        + [shape((tokens, feat), f32), shape((tokens, 1), f32), shape((tokens, 2 * tokens), bf)]
-        + [shape((2 * tokens, feat), bf)] * 2
-        + [shape((8, feat), f32)],
-        scratch_shapes=[pltpu.VMEM((tokens, feat), bf)],
-        compiler_params=pltpu.CompilerParams(vmem_limit_bytes=VMEM_CAP),
-        name="attend",
-    )(x, gain, wq, wk, wv, wo, cents, routes, prefix, cotangent)
+        functools.partial(front_kernel, zs, heads),
+        out_shape=shapes,
+        in_specs=[vm] * 8 + [pl.BlockSpec(memory_space=pltpu.SMEM)],
+        out_specs=[hbm] * 4 + [vm] * 13,
+        scratch_shapes=[pltpu.VMEM(s, bf) for s in wholes]
+        + [
+            pltpu.VMEM((tokens, feat), bf),
+            dma((n,)), dma((n, 2, zs)), dma((n, 2, zs)), dma((n, 2)), dma((n, 2)), dma((n,)), dma((n,)), dma((4,)),
+        ],
+        compiler_params=pltpu.CompilerParams(collective_id=1, has_side_effects=True, vmem_limit_bytes=VMEM_CAP),
+        name="front",
+    )(*shards_in, x, routes, cotangent, prefix)
 
 
 SLICES = 4
@@ -1052,7 +1096,7 @@
         return push(prod.at[w, :, :, 1 - ep], ep_in.at[w], es.at[w], er.at[w], y_peer)
 
     def attn_x(w):
-        return push(prod.at[w, :, 1 - x, ep], x_in.at[w], axs.at[w], axr.at[w], x_peer)
+        return push(prod.at[w, z, 1 - x, ep], x_in.at[w], axs.at[w], axr.at[w], x_peer)
 
     def fold_ep(w):
         attn_ep(w).wait()
@@ -1070,46 +1114,54 @@
         to_right = d > z
         nxt = jnp.where(to_right, z + 1, z - 1)
         slot = jnp.where(d != nxt, d, jnp.where(to_right, d, zs))
-        return push(prod.at[w, d, x, ep], z_in.at[w, slot], azs.at[w, k], azr.at[w, slot], device(nxt, x, core, ep))
+        return push(prod.at[w, d, :, ep], z_in.at[w, slot], azs.at[w, k], azr.at[w, slot], device(nxt, x, core, ep))
 
     def attn_z_wait(w, slot):
         ref = z_in.at[w, slot]
         push(ref, ref, azs.at[w, 0], azr.at[w, slot], x_peer).wait_recv()
-        return ref[...].astype(f32)
-
-    def fold_x(w):
-        attn_x(w).wait()
-
+
+    def begin_z(w):
+        def body(k, carry):
+            @pl.when(begins(dest(k)))
+            def _():
+                attn_z_copy(w, k).start()
+
+            return carry
+
+        lax.fori_loop(0, zs - 1, body, 0)
+
+    def forward_z(w):
         def body(k, carry):
             d = dest(k)
-            total = prod[w, d, x, ep].astype(f32) + x_in[w, d].astype(f32)
-            prod[w, d, x, ep] = total.astype(bf)
-            return carry
-
-        lax.fori_loop(0, zs, body, 0)
-
-    def fold_z(w):
-        def body(k, carry):
-            d = dest(k)
 
             @pl.when(jnp.logical_not(begins(d)))
             def _():
-                total = prod[w, d, x, ep].astype(f32) + attn_z_wait(w, d)
-                prod[w, d, x, ep] = total.astype(bf)
-
-            attn_z_copy(w, k).start()
+                attn_z_wait(w, d)
+                for i in range(2):
+                    prod[w, d, i, ep] = (prod[w, d, i, ep].astype(f32) + z_in[w, d, i].astype(f32)).astype(bf)
+                attn_z_copy(w, k).start()
+
             return carry
 
         lax.fori_loop(0, zs - 1, body, 0)
 
-    def last_z(w):
+    def own_z(w):
         first = jnp.where(z > 0, z, zs)
-        out_a[w][...] = prod[w, z, x, ep].astype(f32) + attn_z_wait(w, first)
+        attn_z_wait(w, first)
+        for i in range(2):
+            prod[w, z, i, ep] = (prod[w, z, i, ep].astype(f32) + z_in[w, first, i].astype(f32)).astype(bf)
 
         @pl.when((z > 0) & (z < zs - 1))
         def _():
-            out_a[w][...] += attn_z_wait(w, zs)
-
+            attn_z_wait(w, zs)
+            for i in range(2):
+                prod[w, z, i, ep] = (prod[w, z, i, ep].astype(f32) + z_in[w, zs, i].astype(f32)).astype(bf)
+
+        attn_x(w).start()
+
+    def last_x(w):
+        attn_x(w).wait()
+        out_a[w][...] = prod[w, z, x, ep].astype(f32) + x_in[w].astype(f32)
         for k in range(zs - 1):
             attn_z_copy(w, k).wait_send()
 
@@ -1140,7 +1192,7 @@
     def event_x(w):
         def act():
             fold_ep(w)
-            attn_x(w).start()
+            begin_z(w)
 
         return act
 
@@ -1158,14 +1210,19 @@
 
     def event_z(w):
         def act():
-            fold_x(w)
-            fold_z(w)
+            forward_z(w)
+
+        return act
+
+    def event_own(w):
+        def act():
+            own_z(w)
 
         return act
 
     def event_last():
         for w in range(4):
-            last_z(w)
+            last_x(w)
         small_all[...] = end3()
 
     pairs = heads // 2
@@ -1187,6 +1244,7 @@
     ]
     steps_at += [(12 + w, event_x(w)) for w in range(4)]
     steps_at += [(14 + w, event_z(w)) for w in range(4)]
+    steps_at += [(16 + w, event_own(w)) for w in range(4)]
 
     def pipeline(t, carry):
         @pl.when(t < blocks)
@@ -1272,8 +1330,8 @@
             vmem((2, 4, tokens, feat), bf),
             vmem((4, zs, 2, 2, per, feat), bf),
             vmem((4, zs, 2, per, feat), bf),
-            vmem((4, zs, per, feat), bf),
-            vmem((4, zs + 1, per, feat), bf),
+            vmem((4, per, feat), bf),
+            vmem((4, zs + 1, 2, per, feat), bf),
             vmem((4, max(zs, 4), 16, feat), f32),
             vmem((16, feat), f32),
             vmem((2, tile, feat), bf),
@@ -1578,14 +1636,9 @@
     tokens, width = inputs.shape
     extra = jnp.concatenate([attn_gain[None, :], centroids.T], axis=0)
     extra = jnp.pad(extra, ((0, 16 - extra.shape[0]), (0, 128 - per)))
-    full = gather_weights(zs, [w_query, w_key, w_value, w_output, extra])
-    mats = [f.reshape(width, width) for f in full[:4]]
-    extras = full[4].reshape(width // per, 16, 128)[:, :3, :per].transpose(1, 0, 2).reshape(3, width)
-    gain, cents = extras[0:1], extras[1:3]
-    attn_in, queries, keys, values, context, hidden, gate, pick, slot_rows, slot_grads, branch_sq = attend(
-        HEADS, inputs, gain, *mats, cents, routes, prefix, cotangent
-    )
-
+    made = front(zs, HEADS, [w_query, w_key, w_value, w_output, extra], inputs, routes, cotangent, prefix)
+    mats = [f.reshape(width, width) for f in made[:4]]
+    attn_in, queries, keys, values, context, hidden, gate, pick, slot_rows, slot_grads, branch_sq, gain, cents = made[4:]
     gain1, gain2 = norm1_gain, norm2_gain
     weights = (up_first, down_first, up_second, down_second)
     in_one, in_two, act_one, slope_one, act_two, slope_two, middle, delta, sub_sq, rows, grads = expert_forward(

time: 395 us -> 378 us (0.957)
  Pallas kernels: 371 us -> 355 us
    pallas_call x2 -> x1, Pallas kernels: 77.3 us -> 67 us  [front(): pl.pallas_call(functools.partial(front_kernel, zs, heads), out_shape=shap...]
    pallas_call x1, Pallas kernels: 246 us -> 241 us  [backward_step(): pl.pallas_call(functools.partial(step_kernel, zs, heads), out_shape=outs,...]
    unnamed x20 -> x19, local copies, waits for them, and re-layouts: 9.57 us -> 9.56 us
where the time goes in v3:
time: 378 us; the launch traced here: 376 us
  Pallas kernels  355 us (94%)
  local copies, waits for them, and re-layouts  16.6 us (4%)
    pallas_call x1, Pallas kernels, backward_step(): pl.pallas_call(functools.partial(step_kernel, zs, heads), out_shape=outs,...  241 us
    pallas_call x1, Pallas kernels, front(): pl.pallas_call(functools.partial(front_kernel, zs, heads), out_shape=shap...  67 us
    pallas_call x1, Pallas kernels, expert_forward(): pl.pallas_call(functools.partial(expert_forward_kernel, tiles), grid=(3,...  47.2 us
    unnamed x19, local copies, waits for them, and re-layouts  9.56 us

profile of v3, /device:TPU:1, one launch (start us, length us, event | category | flops | bytes accessed | tf_op | source)
XLA Modules:
  0.0 376.0 jit_solution(8577281607165951772)
XLA Ops:
  0.6 1.5 copy.31.refs_6_.refs_32_
  2.8 1.3 fusion.5.refs_4_
  4.0 67.0 %front.1 = (bf16[4,2,2,2,32,1024]{5,4,3,2,1,0:T(8,128)(2,1)}, bf16[4,2,2,2,32,1024]{5,4,3,2,1,0:T(8,128)(2,1)}, bf16[4,2,2,2,32,1024]{5,4,3,2,1,0:T(8,128)(2,1)}...) custom-call(bf16[32,1024]{1,0:T(8,128)(2,1)} %refs_0_.2, ...), custom_call_target="tpu_custom_call" | custom-call | tf_op jit(solution)/shard_map/front/pallas_call | solution.py:493
  71.1 47.2 %expert_forward.1 = (bf16[512,1024]{1,0:T(8,128)(2,1)}, bf16[512,1024]{1,0:T(8,128)(2,1)}, bf16[512,4096]{1,0:T(8,128)(2,1)}, bf16[512,4096]{1,0:T(8,128)(2,1)},...) custom-call(bf16[2,256,1024]{2,1,0:T(8,128)(2,1)} %bitcast.36, ...), custom_call_target="tpu_custom_call" | custom-call | tf_op jit(solution)/shard_map/expert_forward/pallas_call | solution.py:226
  118.3 241.1 %backward_step.1 = (f32[4,256,1024]{2,1,0:T(8,128)}, f32[32,1024]{1,0:T(8,128)}, f32[32,1024]{1,0:T(8,128)}, f32[32,1024]{1,0:T(8,128)}, f32[32,1024]{1,0:T(8,12...) custom-call(bf16[256,1024]{1,0:T(8,128)(2,1)} %refs_0_.3, ...), custom_call_target="tpu_custom_call" | custom-call | tf_op jit(solution)/shard_map/backward_step/pallas_call | solution.py:1319
  359.4 3.9 %fusion.6 = (f32[1,256,1024]{2,1,0:T(8,128)}, f32[1,1024,256]{1,2,0:T(8,128)S(1)}, f32[1,256,1024]{2,1,0:T(8,128)}, f32[1,1024,256]{1,2,0:T(8,128)S(1)}) fusion(f32[4,256,1024]{2,1,0:T(8,128)} %get-tuple-element.88), kind=kLoop, calls=%fused_computation.16 | loop fusion | bytes 8388608 | tf_op jit(solution)/shard_map/slice | solution.py:1658
  363.3 0.0 copy-start
  363.3 0.0 copy-start.3
  363.3 0.0 copy-start.2
  363.3 0.0 copy-start.1
  363.3 1.3 copy.33
  364.6 0.0 copy-start.4
  364.6 1.3 copy.34
  365.9 0.8 constant_dynamic-slice_fusion.1
  366.7 0.6 slice_bitcast_fusion.2
  367.3 0.5 slice_bitcast_fusion.3
  367.8 0.8 constant_dynamic-slice_fusion
  368.5 0.5 fusion.7
  369.1 1.0 slice_reduce_fusion
  370.0 0.5 multiply_sqrt_fusion
  370.5 1.9 copy.42
  372.4 0.0 copy-done
  372.4 1.0 copy.43
  373.4 0.0 copy-done.4
  373.4 0.7 copy.44
  374.0 0.0 copy-done.3
  374.0 0.7 copy.45
  374.7 0.0 copy-done.2
  374.7 0.7 copy.46
  375.4 0.0 copy-done.1
  375.4 0.7 copy.47
Async XLA Ops:
  363.3 9.1 %copy-start = (f32[256,1024]{1,0:T(8,128)S(1)}, f32[256,1024]{1,0:T(8,128)}, u32[]{:S(2)}) copy-start(f32[256,1024]{1,0:T(8,128)} %get-tuple-element.126) | copy-start | bytes 3145732
  363.3 10.7 %copy-start.3 = (f32[32,1024]{1,0:T(8,128)S(1)}, f32[32,1024]{1,0:T(8,128)}, u32[]{:S(2)}) copy-start(f32[32,1024]{1,0:T(8,128)} %get-tuple-element.129) | copy-start | bytes 393220
  363.3 11.4 %copy-start.2 = (f32[32,1024]{1,0:T(8,128)S(1)}, f32[32,1024]{1,0:T(8,128)}, u32[]{:S(2)}) copy-start(f32[32,1024]{1,0:T(8,128)} %get-tuple-element.130) | copy-start | bytes 393220
  363.3 12.0 %copy-start.1 = (f32[32,1024]{1,0:T(8,128)S(1)}, f32[32,1024]{1,0:T(8,128)}, u32[]{:S(2)}) copy-start(f32[32,1024]{1,0:T(8,128)} %get-tuple-element.131) | copy-start | bytes 393220
  364.6 8.7 %copy-start.4 = (f32[32,1024]{1,0:T(8,128)S(1)}, f32[32,1024]{1,0:T(8,128)}, u32[]{:S(2)}) copy-start(f32[32,1024]{1,0:T(8,128)} %get-tuple-element.128) | copy-start | bytes 393220

commit v4 on v3

--- a/solution.py
+++ b/solution.py
@@ -505,7 +505,7 @@
     )(*shards_in, x, routes, cotangent, prefix)
 
 
-SLICES = 4
+SLICES = 2
 X_SLICES = 1
 LEAD = 2
 LAG = 3
@@ -1243,8 +1243,8 @@
         (13, event_small3),
     ]
     steps_at += [(12 + w, event_x(w)) for w in range(4)]
-    steps_at += [(14 + w, event_z(w)) for w in range(4)]
-    steps_at += [(16 + w, event_own(w)) for w in range(4)]
+    steps_at += [(13 + w, event_z(w)) for w in range(4)]
+    steps_at += [(15 + w, event_own(w)) for w in range(4)]
 
     def pipeline(t, carry):
         @pl.when(t < blocks)

time: 378 us -> 379 us (level)
  no operation moved by 1% of the time
where the time goes in v4:
time: 379 us; the launch traced here: 377 us
  Pallas kernels  356 us (94%)
  local copies, waits for them, and re-layouts  16.6 us (4%)
    pallas_call x1, Pallas kernels, backward_step(): pl.pallas_call(functools.partial(step_kernel, zs, heads), out_shape=outs,...  242 us
    pallas_call x1, Pallas kernels, front(): pl.pallas_call(functools.partial(front_kernel, zs, heads), out_shape=shap...  67 us
    pallas_call x1, Pallas kernels, expert_forward(): pl.pallas_call(functools.partial(expert_forward_kernel, tiles), grid=(3,...  47.2 us
    unnamed x19, local copies, waits for them, and re-layouts  9.56 us

profile of v4, /device:TPU:1, one launch (start us, length us, event | category | flops | bytes accessed | tf_op | source)
XLA Modules:
  0.0 376.8 jit_solution(11188942729030860779)
XLA Ops:
  0.6 1.5 copy.31.refs_6_.refs_32_
  2.8 1.3 fusion.5.refs_4_
  4.0 67.0 %front.1 = (bf16[4,2,2,2,32,1024]{5,4,3,2,1,0:T(8,128)(2,1)}, bf16[4,2,2,2,32,1024]{5,4,3,2,1,0:T(8,128)(2,1)}, bf16[4,2,2,2,32,1024]{5,4,3,2,1,0:T(8,128)(2,1)}...) custom-call(bf16[32,1024]{1,0:T(8,128)(2,1)} %refs_0_.2, ...), custom_call_target="tpu_custom_call" | custom-call | tf_op jit(solution)/shard_map/front/pallas_call | solution.py:493
  71.1 47.2 %expert_forward.1 = (bf16[512,1024]{1,0:T(8,128)(2,1)}, bf16[512,1024]{1,0:T(8,128)(2,1)}, bf16[512,4096]{1,0:T(8,128)(2,1)}, bf16[512,4096]{1,0:T(8,128)(2,1)},...) custom-call(bf16[2,256,1024]{2,1,0:T(8,128)(2,1)} %bitcast.36, ...), custom_call_target="tpu_custom_call" | custom-call | tf_op jit(solution)/shard_map/expert_forward/pallas_call | solution.py:226
  118.3 241.9 %backward_step.1 = (f32[4,256,1024]{2,1,0:T(8,128)}, f32[32,1024]{1,0:T(8,128)}, f32[32,1024]{1,0:T(8,128)}, f32[32,1024]{1,0:T(8,128)}, f32[32,1024]{1,0:T(8,12...) custom-call(bf16[256,1024]{1,0:T(8,128)(2,1)} %refs_0_.3, ...), custom_call_target="tpu_custom_call" | custom-call | tf_op jit(solution)/shard_map/backward_step/pallas_call | solution.py:1319
  360.2 3.9 %fusion.6 = (f32[1,256,1024]{2,1,0:T(8,128)}, f32[1,1024,256]{1,2,0:T(8,128)S(1)}, f32[1,256,1024]{2,1,0:T(8,128)}, f32[1,1024,256]{1,2,0:T(8,128)S(1)}) fusion(f32[4,256,1024]{2,1,0:T(8,128)} %get-tuple-element.88), kind=kLoop, calls=%fused_computation.16 | loop fusion | bytes 8388608 | tf_op jit(solution)/shard_map/slice | solution.py:1658
  364.1 0.0 copy-start
  364.1 0.0 copy-start.3
  364.1 0.0 copy-start.2
  364.1 0.0 copy-start.1
  364.1 1.3 copy.33
  365.4 0.0 copy-start.4
  365.4 1.3 copy.34
  366.7 0.8 constant_dynamic-slice_fusion.1
  367.5 0.6 slice_bitcast_fusion.2
  368.1 0.5 slice_bitcast_fusion.3
  368.6 0.8 constant_dynamic-slice_fusion
  369.3 0.5 fusion.7
  369.9 1.0 slice_reduce_fusion
  370.8 0.5 multiply_sqrt_fusion
  371.3 1.9 copy.42
  373.2 0.0 copy-done
  373.2 1.0 copy.43
  374.2 0.0 copy-done.4
  374.2 0.7 copy.44
  374.8 0.0 copy-done.3
  374.8 0.7 copy.45
  375.5 0.0 copy-done.2
  375.5 0.7 copy.46
  376.2 0.0 copy-done.1
  376.2 0.7 copy.47
Async XLA Ops:
  364.1 9.1 %copy-start = (f32[256,1024]{1,0:T(8,128)S(1)}, f32[256,1024]{1,0:T(8,128)}, u32[]{:S(2)}) copy-start(f32[256,1024]{1,0:T(8,128)} %get-tuple-element.126) | copy-start | bytes 3145732
  364.1 10.7 %copy-start.3 = (f32[32,1024]{1,0:T(8,128)S(1)}, f32[32,1024]{1,0:T(8,128)}, u32[]{:S(2)}) copy-start(f32[32,1024]{1,0:T(8,128)} %get-tuple-element.129) | copy-start | bytes 393220
  364.1 11.4 %copy-start.2 = (f32[32,1024]{1,0:T(8,128)S(1)}, f32[32,1024]{1,0:T(8,128)}, u32[]{:S(2)}) copy-start(f32[32,1024]{1,0:T(8,128)} %get-tuple-element.130) | copy-start | bytes 393220
  364.1 12.0 %copy-start.1 = (f32[32,1024]{1,0:T(8,128)S(1)}, f32[32,1024]{1,0:T(8,128)}, u32[]{:S(2)}) copy-start(f32[32,1024]{1,0:T(8,128)} %get-tuple-element.131) | copy-start | bytes 393220
  365.4 8.7 %copy-start.4 = (f32[32,1024]{1,0:T(8,128)S(1)}, f32[32,1024]{1,0:T(8,128)}, u32[]{:S(2)}) copy-start(f32[32,1024]{1,0:T(8,128)} %get-tuple-element.128) | copy-start | bytes 393220
